TPU v7x, 32 devices: a whole 2x2x4 slice. The times are simulated.
32 devices in a mesh: gx: 4 (over y, core), gy: 8 (over z, x).
Axes of the slice: x: 2, y: 2, z: 4, core: 2. Of those that a mesh axis runs over, the one named last changes fastest.
Arguments:
- a_tiles: bfloat16 [4, 8, 16, 27, 128, 128], P('gx', 'gy'), may hold values from -0.5 to 0.5
- p_tiles: bfloat16 [4, 8, 16, 128, 128], P('gx', 'gy'), may hold values from -1.5 to 1.5
- neighbours: int32 [4, 8, 16, 27], P('gx', 'gy'), may hold values from 0 to 143, as said below
- groups: int32 [4, 8, 16, 27], P('gx', 'gy'), may hold values from 0 to 7
- slots: int32 [4, 8, 16, 8], P('gx', 'gy'), may hold values from 0 to 26
- aggregates: int32 [4, 8, 16], P('gx', 'gy'), may hold values from 0 to 31, as said below
Outputs:
- coarse_tiles: float32 [4, 8, 4, 27, 128, 128], P('gx', 'gy')
Inputs may be any that keep to these rules, and one draw needn't show every extreme that they name: `neighbours`: tile k of a fine row on device (x, y) names row q % 16 of device (x + q // 48 - 1, y + (q // 16) % 3 - 1), which is always on the mesh; tile 0 names the row itself. The owner of aggregate g is gy index g // 4, as its coarse row g % 4. At most 4 fine rows of one device have aggregates with one owner; in every slab one owner gets exactly 4 from every device of the slab.
All inputs are finite; a program needn't handle non-finite values.
Results may differ from a plain program's by a relative error of at most 0.005.
Values may be sent and summed in bfloat16 or wider, within the bound.
A program may use at most 128 MiB of HBM per device.

v0:
```python
import jax
import jax.numpy as jnp
from jax import lax
from jax.sharding import PartitionSpec as P

KC = 27
AGG = 4


def extended(block, sides, width):
    for axis, dim in sides:
        count = lax.axis_size(axis)
        forward = [(i, i + 1) for i in range(count - 1)]
        backward = [(target, source) for source, target in forward]
        low = lax.ppermute(
            lax.slice_in_dim(block, block.shape[dim] - width, None, axis=dim), axis, forward
        )
        high = lax.ppermute(lax.slice_in_dim(block, 0, width, axis=dim), axis, backward)
        block = jnp.concatenate([low, block, high], axis=dim)
    return block


def shards(a_tiles, p_tiles, neighbours, groups, slots, aggregates):
    row_count = a_tiles.shape[2]
    tile_size = a_tiles.shape[-1]
    touched = slots.shape[-1]
    owner_count = lax.axis_size("gy")
    row_cap = (2 * row_count + owner_count - 1) // owner_count
    slot_total = owner_count * row_cap
    coarse_rows = row_count // AGG
    a_local = a_tiles[0, 0]
    p_local = p_tiles[0, 0]
    column_local = neighbours[0, 0]
    group_local = groups[0, 0]
    slot_local = slots[0, 0]
    aggregate_local = aggregates[0, 0]
    padded = extended(p_tiles, (("gx", 0), ("gy", 1)), 1)
    p_table = padded.reshape(9 * row_count, tile_size, tile_size)

    def one_row(inputs):
        a_row, column_row, group_row, p_row = inputs
        far_tiles = jnp.take(p_table, column_row, axis=0)
        products = jnp.einsum("kab,kbc->kac", a_row, far_tiles, preferred_element_type=jnp.float32)
        picker = (group_row[:, None] == jnp.arange(touched, dtype=jnp.int32)[None, :]).astype(
            jnp.float32
        )
        summed = jnp.einsum(
            "kf,kac->fac", picker, products, precision=lax.Precision.HIGHEST
        ).astype(jnp.bfloat16)
        return jnp.einsum("ba,fbc->fac", p_row, summed, preferred_element_type=jnp.float32).astype(
            jnp.bfloat16
        )

    partials = lax.map(one_row, (a_local, column_local, group_local, p_local))
    owners = aggregate_local // coarse_rows
    local_row = aggregate_local % coarse_rows
    indices = jnp.arange(row_count, dtype=jnp.int32)
    same_owner = owners[:, None] == owners[None, :]
    earlier = indices[:, None] > indices[None, :]
    ranking = jnp.sum((same_owner & earlier).astype(jnp.int32), axis=1)
    position = owners * row_cap + ranking
    selector = jnp.arange(slot_total, dtype=jnp.int32)[:, None] == position[None, :]
    meta_ints = jnp.concatenate([(local_row + 1)[:, None], slot_local], axis=1)
    meta_sent = jnp.dot(selector.astype(jnp.int32), meta_ints)
    send_tiles = jnp.einsum(
        "sr,rfab->sfab", selector.astype(jnp.bfloat16), partials, preferred_element_type=jnp.float32
    ).astype(jnp.bfloat16)
    recv_contrib, recv_meta = (
        lax.all_to_all(send_tiles, "gy", split_axis=0, concat_axis=0, tiled=True),
        lax.all_to_all(meta_sent, "gy", split_axis=0, concat_axis=0, tiled=True),
    )
    recv_row = recv_meta[:, 0] - 1
    segment_ids = jnp.where(
        recv_row[:, None] >= 0, recv_row[:, None] * KC + recv_meta[:, 1:], coarse_rows * KC
    )
    flat_contrib = recv_contrib.reshape(slot_total * touched, tile_size, tile_size).astype(
        jnp.float32
    )
    coarse = jax.ops.segment_sum(
        flat_contrib, segment_ids.reshape(-1), num_segments=coarse_rows * KC + 1
    )
    coarse = coarse[: coarse_rows * KC]
    return coarse.reshape(1, 1, coarse_rows, KC, tile_size, tile_size)


def solution(mesh):
    return jax.shard_map(
        shards,
        mesh=mesh,
        in_specs=(
            P("gx", "gy", None, None, None, None),
            P("gx", "gy", None, None, None),
            P("gx", "gy", None, None),
            P("gx", "gy", None, None),
            P("gx", "gy", None, None),
            P("gx", "gy", None),
        ),
        out_specs=P("gx", "gy", None, None, None, None),
        check_vma=False,
    )
```

profile of v0, /device:TPU:9, one launch (start us, length us, event | category | flops | bytes accessed | tf_op | source)
XLA Modules:
  0.0 535.9 jit_solution(3211491766969522119)
XLA Ops:
  0.0 3.7 collective-permute-start
  3.7 1.9 collective-permute-start.1
  5.6 4.5 collective-permute-done
  11.3 3.4 collective-permute-done.1
  14.8 3.1 collective-permute-start.2
  17.9 3.1 collective-permute-start.3
  24.7 6.0 %all-to-all-start = ((s32[8,4,9]{2,1,0:T(4,128)}), s32[8,4,9]{2,1,0:T(4,128)S(1)}, u32[]{:S(2)}, u32[]{:S(2)}) async-start(s32[8,4,9]{2,1,0:T(4,128)} %bitcast.13), calls=%async_computation | async-start | bytes 32768 | tf_op jit(solution)/shard_map/all_to_all | solution.py:70
  30.7 48.8 %collective-permute-done.2 = bf16[3,1,16,128,128]{4,3,2,1,0:T(8,128)(2,1)S(1)} collective-permute-done((bf16[3,1,16,128,128]{4,3,2,1,0:T(8,128)(2,1)S(1)}, bf16[3,1,16,128,128]{4,3,2,1,0:T(8,128)(2,1)S(1)}, u32[]{:S(2)}, u32[]{:S(2)}) %collective-permute-start.2) | collective-permute-done | bytes 1572896 | tf_op jit(solution)/shard_map/ppermute | solution.py:15
  79.5 1.9 collective-permute-done.3
  81.3 3.6 pad_maximum_fusion
  84.9 164.5 %while.10 = (s32[]{:T(128)}, bf16[16,8,128,128]{2,3,1,0:T(8,128)(2,1)}, s32[16,27]{1,0:T(8,128)}, bf16[16,27,128,128]{3,2,1,0:T(8,128)(2,1)}, s32[16,27]{1,0:T(8...) while((s32[]{:T(128)}, bf16[16,8,128,128]{2,3,1,0:T(8,128)(2,1)}, ...), condition=%wide.region_2.3_spmd, body=%wide.region_1.2_spmd.sunk | while | flops 189973952 | bytes 7903735 | solution.py:54
  85.6 3.1 gather_fusion
  91.7 1.7 fusion.58
  95.9 3.1 gather_fusion
  102.0 1.7 fusion.58
  106.1 3.1 gather_fusion
  112.2 1.7 fusion.58
  116.4 3.1 gather_fusion
  122.5 1.7 fusion.58
  126.7 3.1 gather_fusion
  132.8 1.7 fusion.58
  137.0 3.1 gather_fusion
  143.1 1.7 fusion.58
  147.3 3.1 gather_fusion
  153.4 1.7 fusion.58
  157.6 3.1 gather_fusion
  163.7 1.7 fusion.58
  167.8 3.1 gather_fusion
  175.7 1.8 fusion.59
  178.1 3.1 gather_fusion
  184.2 1.7 fusion.58
  188.4 3.1 gather_fusion
  198.7 3.1 gather_fusion
  209.0 3.1 gather_fusion
  219.3 3.1 gather_fusion
  229.6 3.1 gather_fusion
  235.7 1.7 fusion.58
  239.8 3.1 gather_fusion
  245.9 1.7 fusion.58
  249.4 6.7 %copy.24 = bf16[16,8,128,128]{3,0,2,1:T(8,128)(2,1)} copy(bf16[16,8,128,128]{2,3,1,0:T(8,128)(2,1)} %get-tuple-element.42) | data formatting | bytes 8388608 | tf_op jit(solution)/shard_map/while | solution.py:54
  256.1 7.8 %convolution_convert_fusion.1 = bf16[32,8,128,128]{3,0,2,1:T(8,128)(2,1)} fusion(bf16[16,8,128,128]{3,0,2,1:T(8,128)(2,1)} %copy.24, s32[16]{0:T(128)S(1)} %multiply_add_fusion), kind=kOutput, calls=%fused_computation.32 | convolution fusion | flops 138412544 | bytes 12582976 | tf_op jit(solution)/shard_map/sr,rfab->sfab/dot_general | solution.py:65
  263.9 9.8 %copy.25 = bf16[32,8,128,128]{3,2,1,0:T(8,128)(2,1)} copy(bf16[32,8,128,128]{3,0,2,1:T(8,128)(2,1)} %convolution_convert_fusion.1) | data formatting | bytes 16777216 | tf_op jit(solution)/shard_map/convert_element_type | solution.py:67
  273.8 5.1 all-to-all-start.1
  279.3 181.1 %all-to-all-done.1 = bf16[32,8,128,128]{3,2,1,0:T(8,128)(2,1)} async-done(((bf16[32,8,128,128]{3,2,1,0:T(8,128)(2,1)}), bf16[32,8,128,128]{3,2,1,0:T(8,128)(2,1)}, u32[]{:S(2)}, u32[]{:S(2)}) %all-to-all-start.1) | async-done | bytes 8388640 | tf_op jit(solution)/shard_map/all_to_all | solution.py:69
  460.4 11.2 %bitcast_convert_fusion = f32[256,128,128]{2,1,0:T(8,128)} fusion(bf16[32,8,128,128]{3,2,1,0:T(8,128)(2,1)} %all-to-all-done.1), kind=kLoop, calls=%fused_computation.31 | loop fusion | flops 4194304 | bytes 25165824 | tf_op jit(solution)/shard_map/convert_element_type | solution.py:76
  471.6 3.8 broadcast_in_dim.45
  475.4 53.6 %scatter_fusion = f32[109,128,128]{2,1,0:T(8,128)} fusion(f32[109,128,128]{2,1,0:T(8,128)} %broadcast_in_dim.45, s32[256]{0:T(256)S(1)} %reshape.186, f32[256,128,128]{2,1,0:T(8,128)} %bitcast_convert_fusion), kind=kCustom, calls=%fused_computation.1 | custom fusion | flops 4194304 | bytes 50332672 | tf_op jit(solution)/shard_map/scatter-add | solution.py:79
  529.0 6.9 %slice.16 = f32[108,128,128]{2,1,0:T(8,128)} slice(f32[109,128,128]{2,1,0:T(8,128)} %scatter_fusion), slice={[0:108], [0:128], [0:128]} | slice | bytes 14155776 | tf_op jit(solution)/shard_map/slice | solution.py:82
  (114 shorter events, 99.8 us)
Async XLA Ops:
  0.0 10.1 %collective-permute-start = (bf16[1,1,16,128,128]{4,3,2,1,0:T(8,128)(2,1)}, bf16[1,1,16,128,128]{4,3,2,1,0:T(8,128)(2,1)S(1)}, u32[]{:S(2)}, u32[]{:S(2)}) collective-permute-start(bf16[1,1,16,128,128]{4,3,2,1,0:T(8,128)(2,1)} %param.9), channel_id=1, source_target_pairs={{0,8},{8,16},{16,24},{1,9},{9,17},{17,25},{2,10},{10,18},{18,26},{... | collective-permute-start | bytes 1572872 | tf_op jit(solution)/shard_map/ppermute | solution.py:15
  3.7 11.0 %collective-permute-start.1 = (bf16[1,1,16,128,128]{4,3,2,1,0:T(8,128)(2,1)}, bf16[1,1,16,128,128]{4,3,2,1,0:T(8,128)(2,1)S(1)}, u32[]{:S(2)}, u32[]{:S(2)}) collective-permute-start(bf16[1,1,16,128,128]{4,3,2,1,0:T(8,128)(2,1)} %param.9), channel_id=1, source_target_pairs={{8,0},{16,8},{24,16},{9,1},{17,9},{25,17},{10,2},{18,10},{26,18},{... | collective-permute-start | bytes 1572872 | tf_op jit(solution)/shard_map/ppermute | solution.py:18
  14.8 64.7 %collective-permute-start.2 = (bf16[3,1,16,128,128]{4,3,2,1,0:T(8,128)(2,1)S(1)}, bf16[3,1,16,128,128]{4,3,2,1,0:T(8,128)(2,1)S(1)}, u32[]{:S(2)}, u32[]{:S(2)}) collective-permute-start(bf16[3,1,16,128,128]{4,3,2,1,0:T(8,128)(2,1)S(1)} %constant_dynamic-update-slice_fusion), channel_id=1, source_target_pairs={{0,1},{1,2},{2,3},{3,4},{4,5},{5,6},{6,7},{8,9},{9,10},{10,11},{11... | collective-permute-start | bytes 4718600 | tf_op jit(solution)/shard_map/ppermute | solution.py:15
  17.9 63.4 %collective-permute-start.3 = (bf16[3,1,16,128,128]{4,3,2,1,0:T(8,128)(2,1)S(1)}, bf16[3,1,16,128,128]{4,3,2,1,0:T(8,128)(2,1)}, u32[]{:S(2)}, u32[]{:S(2)}) collective-permute-start(bf16[3,1,16,128,128]{4,3,2,1,0:T(8,128)(2,1)S(1)} %constant_dynamic-update-slice_fusion), channel_id=1, source_target_pairs={{1,0},{2,1},{3,2},{4,3},{5,4},{6,5},{7,6},{9,8},{10,9},{11,10},{12... | collective-permute-start | bytes 4718600 | tf_op jit(solution)/shard_map/ppermute | solution.py:18
  24.7 249.1 %all-to-all-start = ((s32[8,4,9]{2,1,0:T(4,128)}), s32[8,4,9]{2,1,0:T(4,128)S(1)}, u32[]{:S(2)}, u32[]{:S(2)}) async-start(s32[8,4,9]{2,1,0:T(4,128)} %bitcast.13), calls=%async_computation | async-start | bytes 32768 | tf_op jit(solution)/shard_map/all_to_all | solution.py:70
  273.8 186.6 %all-to-all-start.1 = ((bf16[32,8,128,128]{3,2,1,0:T(8,128)(2,1)}), bf16[32,8,128,128]{3,2,1,0:T(8,128)(2,1)}, u32[]{:S(2)}, u32[]{:S(2)}) async-start(bf16[32,8,128,128]{3,2,1,0:T(8,128)(2,1)} %copy.25), calls=%async_computation.1 | async-start | bytes 16777216 | tf_op jit(solution)/shard_map/all_to_all | solution.py:69
where the time goes:
time: 543 us; the launch traced here: 536 us
  waiting for transfers between devices  240 us (44%)
  other arithmetic  93.3 us (17%)
  matrix products  91.1 us (17%)
  local copies, waits for them, and re-layouts  88.6 us (16%)
  starting transfers between devices  22.9 us (4%)
    all_to_all x1, waiting for transfers between devices, shards(): lax.all_to_all(send_tiles, 'gy', split_axis=0, concat_axis=0, tiled=True)  181 us
    scatter-add x1, other arithmetic, shards(): jax.ops.segment_sum(flat_contrib, segment_ids.reshape(-1), num_segments=c...  53.6 us
    ppermute x2, waiting for transfers between devices, extended(): lax.ppermute(lax.slice_in_dim(block, block.shape[dim] - width, None, axis...  53.2 us
    gather x16, local copies, waits for them, and re-layouts, one_row(): far_tiles = jnp.take(p_table, column_row, axis=0)  48.9 us
    dot_general x16, matrix products, one_row(): jnp.einsum('kf,kac->fac', picker, products, precision=lax.Precision.HIGHEST)  28 us
    dot_general x16, matrix products, one_row(): jnp.einsum('ba,fbc->fac', p_row, summed, preferred_element_type=jnp.float32)  27.7 us
    dot_general x16, matrix products, one_row(): jnp.einsum('kab,kbc->kac', a_row, far_tiles, preferred_element_type=jnp.f...  26 us
    and x16, other arithmetic, one_row(): far_tiles = jnp.take(p_table, column_row, axis=0)  11.3 us
  transfers between devices with their start and end apart: 6, of which 5 were waited for; matrix products, arithmetic and copies ran while one was open for 37% of the time, Pallas kernels for 0%

commit v1 on v0

v1 whole, which is shorter than its diff:
```python
import functools

import jax
import jax.numpy as jnp
from jax import lax
from jax.experimental import pallas as pl
from jax.experimental.pallas import tpu as pltpu
from jax.sharding import PartitionSpec as P

KC = 27
AGG = 4
CHUNKS = 1


def shifted(block, axis, step):
    count = lax.axis_size(axis)
    pairs = [(i, i + step) for i in range(count) if 0 <= i + step < count]
    return lax.ppermute(block, axis, pairs)


def halo(block):
    below, above = shifted(block, "gy", 1), shifted(block, "gy", -1)
    line = (below, block, above)
    low = [shifted(piece, "gx", 1) for piece in line]
    high = [shifted(piece, "gx", -1) for piece in line]
    return (*low, *line, *high)


def row_kernel(order, place, count, near, group, a_ref, *rest):
    pieces, (out_ref, table, sums, sems) = rest[:9], rest[9:]
    step = pl.program_id(0)
    tiles, rows = a_ref.shape[1], pieces[0].shape[0]
    touched = sums.shape[0]

    @pl.when(step == 0)
    def _():
        copies = [
            pltpu.make_async_copy(piece, table.at[pl.ds(j * rows, rows)], sems.at[j])
            for j, piece in enumerate(pieces)
        ]
        for copy in copies:
            copy.start()
        for copy in copies:
            copy.wait()

    @pl.when(step < count[0])
    def _():
        row = order[step]
        sums[...] = jnp.zeros_like(sums)
        for k in range(tiles):
            product = jnp.dot(
                a_ref[0, k], table[near[row, k]], preferred_element_type=jnp.float32
            )
            sums[group[row, k]] += product
        own = table[4 * rows + row]
        for f in range(touched):
            out_ref[0, f] = lax.dot_general(
                own,
                sums[f].astype(jnp.bfloat16),
                (((0,), (0,)), ((), ())),
                preferred_element_type=jnp.float32,
            ).astype(jnp.bfloat16)


def row_products(a_local, pieces, near, group, order, place, count, slot_total, touched):
    rows, tiles, size, _ = a_local.shape
    steps = order.shape[0]
    flops = 2 * steps * (tiles + touched) * size**3
    return pl.pallas_call(
        row_kernel,
        out_shape=jax.ShapeDtypeStruct((slot_total, touched, size, size), jnp.bfloat16),
        grid_spec=pltpu.PrefetchScalarGridSpec(
            num_scalar_prefetch=5,
            grid=(steps,),
            in_specs=[
                pl.BlockSpec(
                    (1, tiles, size, size), lambda i, order, *_: (order[i], 0, 0, 0)
                )
            ]
            + [pl.BlockSpec(memory_space=pl.ANY)] * 9,
            out_specs=pl.BlockSpec(
                (1, touched, size, size), lambda i, order, place, *_: (place[i], 0, 0, 0)
            ),
            scratch_shapes=[
                pltpu.VMEM((9 * rows, size, size), jnp.bfloat16),
                pltpu.VMEM((touched, size, size), jnp.float32),
                pltpu.SemaphoreType.DMA((9,)),
            ],
        ),
        compiler_params=pltpu.CompilerParams(vmem_limit_bytes=24 << 20),
        cost_estimate=pl.CostEstimate(
            flops=flops, bytes_accessed=2 * steps * (tiles + touched) * size**2, transcendentals=0
        ),
    )(order, place, count, near, group, a_local, *pieces)


def sum_kernel(carried, segment, valid, recv_ref, *rest):
    out_ref = rest[-1]
    step = pl.program_id(0)

    @pl.when(step == 0)
    def _():
        out_ref[...] = rest[0][...] if carried else jnp.zeros_like(out_ref)

    @pl.when(valid[step] > 0)
    def _():
        for f in range(recv_ref.shape[1]):
            out_ref[segment[step, f]] += recv_ref[0, f].astype(jnp.float32)


def coarse_sums(recv, segment, valid, total, previous):
    slot_total, touched, size, _ = recv.shape
    whole = pl.BlockSpec((total, size, size), lambda i, *_: (0, 0, 0), pipeline_mode=pl.Buffered(1))
    carried = previous is not None
    return pl.pallas_call(
        functools.partial(sum_kernel, carried),
        out_shape=jax.ShapeDtypeStruct((total, size, size), jnp.float32),
        grid_spec=pltpu.PrefetchScalarGridSpec(
            num_scalar_prefetch=2,
            grid=(slot_total,),
            in_specs=[pl.BlockSpec((1, touched, size, size), lambda i, *_: (i, 0, 0, 0))]
            + [whole] * carried,
            out_specs=pl.BlockSpec((total, size, size), lambda i, *_: (0, 0, 0)),
        ),
        compiler_params=pltpu.CompilerParams(vmem_limit_bytes=32 << 20),
        cost_estimate=pl.CostEstimate(
            flops=slot_total * touched * size**2,
            bytes_accessed=(2 * slot_total * touched + 4 * total) * size**2,
            transcendentals=0,
        ),
    )(segment, valid, recv, *([previous] if carried else []))


def shards(a_tiles, p_tiles, neighbours, groups, slots, aggregates):
    row_count = a_tiles.shape[2]
    touched = slots.shape[-1]
    size = a_tiles.shape[-1]
    owner_count = lax.axis_size("gy")
    row_cap = (2 * row_count + owner_count - 1) // owner_count
    coarse_rows = row_count // AGG
    total = coarse_rows * KC
    a_local, p_local = a_tiles[0, 0], p_tiles[0, 0]
    near, group = neighbours[0, 0], groups[0, 0]
    slot_local, aggregate = slots[0, 0], aggregates[0, 0]

    owners = aggregate // coarse_rows
    local_row = aggregate % coarse_rows
    indices = jnp.arange(row_count, dtype=jnp.int32)
    same_owner = owners[:, None] == owners[None, :]
    earlier = indices[:, None] > indices[None, :]
    rank = jnp.sum((same_owner & earlier).astype(jnp.int32), axis=1)
    chunks = min(CHUNKS, row_cap)
    width = row_cap // chunks
    position = (rank // width * owner_count + owners) * width + rank % width
    slot_total = owner_count * row_cap
    selector = jnp.arange(slot_total, dtype=jnp.int32)[:, None] == position[None, :]
    segments = local_row[:, None] * KC + slot_local
    meta = jnp.concatenate([jnp.ones_like(local_row)[:, None], segments], axis=1)
    meta_sent = jnp.sum(jnp.where(selector[:, :, None], meta[None], 0), axis=1)
    meta_sent = meta_sent.reshape(chunks, owner_count, width, touched + 1)
    meta_recv = lax.all_to_all(meta_sent, "gy", split_axis=1, concat_axis=1, tiled=True)
    meta_recv = meta_recv.reshape(chunks, owner_count * width, touched + 1)

    pieces = halo(p_local)
    coarse = None
    sent = []
    for chunk in range(chunks):
        steps = min(row_count, owner_count * width, row_count)
        active = rank // width == chunk
        count = jnp.sum(active.astype(jnp.int32))
        ahead = jnp.sum((active[None, :] & earlier).astype(jnp.int32), axis=1)
        wanted = jnp.minimum(jnp.arange(steps, dtype=jnp.int32), count - 1)
        chosen = active[None, :] & (ahead[None, :] == wanted[:, None])
        order = jnp.sum(jnp.where(chosen, indices[None, :], 0), axis=1)
        place = jnp.sum(jnp.where(chosen, (owners * width + rank % width)[None, :], 0), axis=1)
        sent.append(
            row_products(
                a_local, pieces, near, group, order, place, count[None],
                owner_count * width, touched,
            )
        )
    recv = [lax.all_to_all(s, "gy", split_axis=0, concat_axis=0, tiled=True) for s in sent]
    for chunk in range(chunks):
        coarse = coarse_sums(
            recv[chunk], meta_recv[chunk, :, 1:], meta_recv[chunk, :, 0], total, coarse
        )
    return coarse.reshape(1, 1, coarse_rows, KC, size, size)


def solution(mesh):
    return jax.shard_map(
        shards,
        mesh=mesh,
        in_specs=(
            P("gx", "gy", None, None, None, None),
            P("gx", "gy", None, None, None),
            P("gx", "gy", None, None),
            P("gx", "gy", None, None),
            P("gx", "gy", None, None),
            P("gx", "gy", None),
        ),
        out_specs=P("gx", "gy", None, None, None, None),
        check_vma=False,
    )
```

time: 543 us -> 280 us (0.52)
  matrix products: 91.1 us -> 0 us
  other arithmetic: 93.3 us -> 2.67 us
  local copies, waits for them, and re-layouts: 88.6 us -> 11.5 us
  waiting for transfers between devices: 240 us -> 191 us
  Pallas kernels: 0 us -> 33.6 us
  starting transfers between devices: 22.9 us -> 35.5 us
    dot_general x50 -> x0, matrix products: 91.1 us -> none  [the longest x16 28 us: one_row(): jnp.einsum('kf,kac->fac', picker, products, precision=lax.Precision.HIGHEST)]
    scatter-add x1 -> x0, other arithmetic: 53.6 us -> none  [shards(): jax.ops.segment_sum(flat_contrib, segment_ids.reshape(-1), num_segments=c...]
    gather x16 -> x0, local copies, waits for them, and re-layouts: 48.9 us -> none  [one_row(): far_tiles = jnp.take(p_table, column_row, axis=0)]
    ppermute x4 -> x8, waiting for transfers between devices: 58.5 us -> 12.1 us  [shifted(): return lax.ppermute(block, axis, pairs)]
    pallas_call x0 -> x2, Pallas kernels: none -> 33.6 us  [the longest x1 20.2 us: coarse_sums(): pl.pallas_call(functools.partial(sum_kernel, carried), out_shape=jax.Shap...]
    ppermute x4 -> x8, starting transfers between devices: 11.8 us -> 24.4 us  [shifted(): return lax.ppermute(block, axis, pairs)]
    and x16 -> x0, other arithmetic: 11.3 us -> none  [one_row(): far_tiles = jnp.take(p_table, column_row, axis=0)]
    convert_element_type x1 -> x0, other arithmetic: 11.2 us -> none  [shards(): recv_contrib.reshape(slot_total * touched, tile_size, tile_size)]
  transfers between devices with their start and end apart: 6 -> 10, of which waited for: 5 -> 3; matrix products, arithmetic and copies ran while one was open for 37% -> 1% of each run, Pallas kernels for 0% -> 5%
where the time goes in v1:
time: 280 us; the launch traced here: 275 us
  waiting for transfers between devices  191 us (68%)
  starting transfers between devices  35.5 us (13%)
  Pallas kernels  33.6 us (12%)
  local copies, waits for them, and re-layouts  11.5 us (4%)
    all_to_all x1, waiting for transfers between devices, shards(): lax.all_to_all(s, 'gy', split_axis=0, concat_axis=0, tiled=True)  179 us
    ppermute x8, starting transfers between devices, shifted(): return lax.ppermute(block, axis, pairs)  24.4 us
    pallas_call x1, Pallas kernels, coarse_sums(): pl.pallas_call(functools.partial(sum_kernel, carried), out_shape=jax.Shap...  20.2 us
    pallas_call x1, Pallas kernels, row_products(): pl.pallas_call(row_kernel, out_shape=jax.ShapeDtypeStruct((slot_total, to...  13.4 us
    ppermute x8, waiting for transfers between devices, shifted(): return lax.ppermute(block, axis, pairs)  12.1 us
    unnamed x10, local copies, waits for them, and re-layouts  10.7 us
  transfers between devices with their start and end apart: 10, of which 3 were waited for; matrix products, arithmetic and copies ran while one was open for 1% of the time, Pallas kernels for 5%

profile of v1, /device:TPU:9, one launch (start us, length us, event | category | flops | bytes accessed | tf_op | source)
XLA Modules:
  0.0 275.5 jit_solution(2139713022707567198)
XLA Ops:
  0.0 3.1 %collective-permute-start = (bf16[16,128,128]{2,1,0:T(8,128)(2,1)}, bf16[16,128,128]{2,1,0:T(8,128)(2,1)S(1)}, u32[]{:S(2)}, u32[]{:S(2)}) collective-permute-start(bf16[16,128,128]{2,1,0:T(8,128)(2,1)} %bitcast.30), channel_id=1, source_target_pairs={{0,1},{1,2},{2,3},{3,4},{4,5},{5,6},{6,7},{8,9},{9,10},{10,11},{11... | collective-permute-start | bytes 1572872 | tf_op jit(solution)/shard_map/ppermute | solution.py:18
  3.1 3.1 %collective-permute-start.3 = (bf16[16,128,128]{2,1,0:T(8,128)(2,1)}, bf16[16,128,128]{2,1,0:T(8,128)(2,1)S(1)}, u32[]{:S(2)}, u32[]{:S(2)}) collective-permute-start(bf16[16,128,128]{2,1,0:T(8,128)(2,1)} %bitcast.31), channel_id=1, source_target_pairs={{1,0},{2,1},{3,2},{4,3},{5,4},{6,5},{7,6},{9,8},{10,9},{11,10},{12... | collective-permute-start | bytes 1572872 | tf_op jit(solution)/shard_map/ppermute | solution.py:18
  6.2 4.3 %collective-permute-start.2 = (bf16[16,128,128]{2,1,0:T(8,128)(2,1)}, bf16[16,128,128]{2,1,0:T(8,128)(2,1)S(1)}, u32[]{:S(2)}, u32[]{:S(2)}) collective-permute-start(bf16[16,128,128]{2,1,0:T(8,128)(2,1)} %bitcast.32), channel_id=1, source_target_pairs={{0,8},{8,16},{16,24},{1,9},{9,17},{17,25},{2,10},{10,18},{18,26},{... | collective-permute-start | bytes 1572872 | tf_op jit(solution)/shard_map/ppermute | solution.py:18
  10.5 1.9 collective-permute-start.6
  12.4 0.7 and_select_fusion.3
  13.1 0.2 convert_reduce_fusion.1
  13.2 0.7 bitcast_add_fusion
  13.9 0.6 convert_reduce_fusion.2
  15.2 0.1 iota_compare_fusion.1
  15.3 10.0 %collective-permute-done.rest_3_ = bf16[16,128,128]{2,1,0:T(8,128)(2,1)S(1)} collective-permute-done((bf16[16,128,128]{2,1,0:T(8,128)(2,1)}, bf16[16,128,128]{2,1,0:T(8,128)(2,1)S(1)}, u32[]{:S(2)}, u32[]{:S(2)}) %collective-permute-start) | collective-permute-done | bytes 524320 | tf_op jit(solution)/shard_map/ppermute | solution.py:18
  25.3 4.6 %collective-permute-start.1 = (bf16[16,128,128]{2,1,0:T(8,128)(2,1)S(1)}, bf16[16,128,128]{2,1,0:T(8,128)(2,1)S(1)}, u32[]{:S(2)}, u32[]{:S(2)}) collective-permute-start(bf16[16,128,128]{2,1,0:T(8,128)(2,1)S(1)} %collective-permute-done.rest_3_), channel_id=1, source_target_pairs={{0,8},{8,16},{16,24},{1,9},{9,17},{17,25},{2,10},{10,18},{18,26},{... | collective-permute-start | bytes 1572872 | tf_op jit(solution)/shard_map/ppermute | solution.py:18
  29.8 1.9 collective-permute-start.5
  31.7 0.0 collective-permute-done.3.rest_5_
  31.8 3.6 %collective-permute-start.4 = (bf16[16,128,128]{2,1,0:T(8,128)(2,1)S(1)}, bf16[16,128,128]{2,1,0:T(8,128)(2,1)}, u32[]{:S(2)}, u32[]{:S(2)}) collective-permute-start(bf16[16,128,128]{2,1,0:T(8,128)(2,1)S(1)} %collective-permute-done.3.rest_5_), channel_id=1, source_target_pairs={{0,8},{8,16},{16,24},{1,9},{9,17},{17,25},{2,10},{10,18},{18,26},{... | collective-permute-start | bytes 1572872 | tf_op jit(solution)/shard_map/ppermute | solution.py:18
  35.4 0.0 collective-permute-done.2.rest_1_
  35.4 1.9 collective-permute-start.7
  37.3 0.1 select_reduce_fusion
  37.4 0.7 copy.11
  38.1 5.6 %all-to-all-start = ((s32[1,8,4,9]{3,2,0,1:T(4,128)}), s32[1,8,4,9]{3,2,0,1:T(4,128)S(1)}, u32[]{:S(2)}, u32[]{:S(2)}) async-start(s32[1,8,4,9]{3,2,0,1:T(4,128)} %bitcast.3), calls=%async_computation | async-start | bytes 32768 | tf_op jit(solution)/shard_map/all_to_all | solution.py:161
  43.7 0.1 convert_reduce_fusion
  43.8 0.2 select_reduce_fusion.1
  44.0 0.0 collective-permute-done.6.rest_7_
  44.0 0.0 collective-permute-done.1.rest_0_
  44.0 0.0 collective-permute-done.4.rest_2_
  44.0 0.0 collective-permute-done.5.rest_6_
  44.0 2.0 collective-permute-done.7.rest_8_
  46.1 0.0 copy-start.1
  46.1 5.0 %copy-done.1 = bf16[1,1,16,27,128,128]{5,4,3,2,1,0:T(8,128)(2,1)S(1)} copy-done((bf16[1,1,16,27,128,128]{5,4,3,2,1,0:T(8,128)(2,1)S(1)}, bf16[1,1,16,27,128,128]{5,4,3,2,1,0:T(8,128)(2,1)}, u32[]{:S(2)}) %copy-start.1) | copy-done | bytes 14155800
  51.1 0.0 copy-start.2
  51.1 1.0 copy-done.2
  52.2 0.0 copy-start.3
  52.2 0.7 copy-done.3
  52.9 0.0 copy-start.4
  52.9 0.7 copy-done.4
  53.6 13.4 %shard_map.64 = bf16[32,8,128,128]{3,2,1,0:T(8,128)(2,1)S(1)} custom-call(s32[16]{0:T(128)S(1)} %get-tuple-element.6.order, s32[16]{0:T(128)S(1)} %get-tuple-element.5.place, s32[1]{0:T(128)} %bitcast.6.count, s32[16,27]{1,0:T(8,128)S(1)} %bitcast.35, s32[16,27]{1,0:T(8,128)S(1)} %bitcast.36, bf16[16,27,128,128]{3,2,1,0:T(8,128)(2,1)S(1)} %bitcast.29, ...), custom_call_target="tpu_custom_call" | custom-call | flops 2348810240 | bytes 18350080 | tf_op jit(solution)/shard_map/pallas_call | solution.py:69
  67.0 0.0 copy-start
  67.0 3.2 %copy-done = bf16[32,8,128,128]{3,2,1,0:T(8,128)(2,1)} copy-done((bf16[32,8,128,128]{3,2,1,0:T(8,128)(2,1)}, bf16[32,8,128,128]{3,2,1,0:T(8,128)(2,1)S(1)}, u32[]{:S(2)}) %copy-start) | copy-done | bytes 8388632
  70.2 0.0 all-to-all-done
  70.2 5.5 %all-to-all-start.1 = ((bf16[32,8,128,128]{3,2,1,0:T(8,128)(2,1)}), bf16[32,8,128,128]{3,2,1,0:T(8,128)(2,1)}, u32[]{:S(2)}, u32[]{:S(2)}) async-start(bf16[32,8,128,128]{3,2,1,0:T(8,128)(2,1)} %copy-done), calls=%async_computation.1 | async-start | bytes 16777216 | tf_op jit(solution)/shard_map/all_to_all | solution.py:182
  75.7 0.1 slice_reduce_fusion.valid
  75.8 0.1 slice_bitcast_fusion.segment
  75.9 179.4 %all-to-all-done.1.recv_ref = bf16[32,8,128,128]{3,2,1,0:T(8,128)(2,1)} async-done(((bf16[32,8,128,128]{3,2,1,0:T(8,128)(2,1)}), bf16[32,8,128,128]{3,2,1,0:T(8,128)(2,1)}, u32[]{:S(2)}, u32[]{:S(2)}) %all-to-all-start.1) | async-done | bytes 8388640 | tf_op jit(solution)/shard_map/all_to_all | solution.py:182
  255.3 20.2 %shard_map.65 = f32[108,128,128]{2,1,0:T(8,128)} custom-call(s32[32,8]{1,0:T(8,128)S(1)} %slice_bitcast_fusion.segment, s32[32]{0:T(128)S(1)} %slice_reduce_fusion.valid, bf16[32,8,128,128]{3,2,1,0:T(8,128)(2,1)} %all-to-all-done.1.recv_ref), custom_call_target="tpu_custom_call" | custom-call | flops 4194304 | bytes 15466496 | tf_op jit(solution)/shard_map/pallas_call | solution.py:115
  (3 shorter events, 0.0 us)
Async XLA Ops:
  0.0 25.3 %collective-permute-start = (bf16[16,128,128]{2,1,0:T(8,128)(2,1)}, bf16[16,128,128]{2,1,0:T(8,128)(2,1)S(1)}, u32[]{:S(2)}, u32[]{:S(2)}) collective-permute-start(bf16[16,128,128]{2,1,0:T(8,128)(2,1)} %bitcast.30), channel_id=1, source_target_pairs={{0,1},{1,2},{2,3},{3,4},{4,5},{5,6},{6,7},{8,9},{9,10},{10,11},{11... | collective-permute-start | bytes 1572872 | tf_op jit(solution)/shard_map/ppermute | solution.py:18
  3.1 28.6 %collective-permute-start.3 = (bf16[16,128,128]{2,1,0:T(8,128)(2,1)}, bf16[16,128,128]{2,1,0:T(8,128)(2,1)S(1)}, u32[]{:S(2)}, u32[]{:S(2)}) collective-permute-start(bf16[16,128,128]{2,1,0:T(8,128)(2,1)} %bitcast.31), channel_id=1, source_target_pairs={{1,0},{2,1},{3,2},{4,3},{5,4},{6,5},{7,6},{9,8},{10,9},{11,10},{12... | collective-permute-start | bytes 1572872 | tf_op jit(solution)/shard_map/ppermute | solution.py:18
  6.2 29.2 %collective-permute-start.2 = (bf16[16,128,128]{2,1,0:T(8,128)(2,1)}, bf16[16,128,128]{2,1,0:T(8,128)(2,1)S(1)}, u32[]{:S(2)}, u32[]{:S(2)}) collective-permute-start(bf16[16,128,128]{2,1,0:T(8,128)(2,1)} %bitcast.32), channel_id=1, source_target_pairs={{0,8},{8,16},{16,24},{1,9},{9,17},{17,25},{2,10},{10,18},{18,26},{... | collective-permute-start | bytes 1572872 | tf_op jit(solution)/shard_map/ppermute | solution.py:18
  10.5 33.5 %collective-permute-start.6 = (bf16[16,128,128]{2,1,0:T(8,128)(2,1)}, bf16[16,128,128]{2,1,0:T(8,128)(2,1)S(1)}, u32[]{:S(2)}, u32[]{:S(2)}) collective-permute-start(bf16[16,128,128]{2,1,0:T(8,128)(2,1)} %bitcast.33), channel_id=1, source_target_pairs={{8,0},{16,8},{24,16},{9,1},{17,9},{25,17},{10,2},{18,10},{26,18},{... | collective-permute-start | bytes 1572872 | tf_op jit(solution)/shard_map/ppermute | solution.py:18
  25.3 18.8 %collective-permute-start.1 = (bf16[16,128,128]{2,1,0:T(8,128)(2,1)S(1)}, bf16[16,128,128]{2,1,0:T(8,128)(2,1)S(1)}, u32[]{:S(2)}, u32[]{:S(2)}) collective-permute-start(bf16[16,128,128]{2,1,0:T(8,128)(2,1)S(1)} %collective-permute-done.rest_3_), channel_id=1, source_target_pairs={{0,8},{8,16},{16,24},{1,9},{9,17},{17,25},{2,10},{10,18},{18,26},{... | collective-permute-start | bytes 1572872 | tf_op jit(solution)/shard_map/ppermute | solution.py:18
  29.8 14.2 %collective-permute-start.5 = (bf16[16,128,128]{2,1,0:T(8,128)(2,1)S(1)}, bf16[16,128,128]{2,1,0:T(8,128)(2,1)S(1)}, u32[]{:S(2)}, u32[]{:S(2)}) collective-permute-start(bf16[16,128,128]{2,1,0:T(8,128)(2,1)S(1)} %collective-permute-done.rest_3_), channel_id=1, source_target_pairs={{8,0},{16,8},{24,16},{9,1},{17,9},{25,17},{10,2},{18,10},{26,18},{... | collective-permute-start | bytes 1572872 | tf_op jit(solution)/shard_map/ppermute | solution.py:18
  31.8 12.3 %collective-permute-start.4 = (bf16[16,128,128]{2,1,0:T(8,128)(2,1)S(1)}, bf16[16,128,128]{2,1,0:T(8,128)(2,1)}, u32[]{:S(2)}, u32[]{:S(2)}) collective-permute-start(bf16[16,128,128]{2,1,0:T(8,128)(2,1)S(1)} %collective-permute-done.3.rest_5_), channel_id=1, source_target_pairs={{0,8},{8,16},{16,24},{1,9},{9,17},{17,25},{2,10},{10,18},{18,26},{... | collective-permute-start | bytes 1572872 | tf_op jit(solution)/shard_map/ppermute | solution.py:18
  35.4 10.7 %collective-permute-start.7 = (bf16[16,128,128]{2,1,0:T(8,128)(2,1)S(1)}, bf16[16,128,128]{2,1,0:T(8,128)(2,1)}, u32[]{:S(2)}, u32[]{:S(2)}) collective-permute-start(bf16[16,128,128]{2,1,0:T(8,128)(2,1)S(1)} %collective-permute-done.3.rest_5_), channel_id=1, source_target_pairs={{8,0},{16,8},{24,16},{9,1},{17,9},{25,17},{10,2},{18,10},{26,18},{... | collective-permute-start | bytes 1572872 | tf_op jit(solution)/shard_map/ppermute | solution.py:18
  38.1 32.1 %all-to-all-start = ((s32[1,8,4,9]{3,2,0,1:T(4,128)}), s32[1,8,4,9]{3,2,0,1:T(4,128)S(1)}, u32[]{:S(2)}, u32[]{:S(2)}) async-start(s32[1,8,4,9]{3,2,0,1:T(4,128)} %bitcast.3), calls=%async_computation | async-start | bytes 32768 | tf_op jit(solution)/shard_map/all_to_all | solution.py:161
  46.1 5.0 %copy-start.1 = (bf16[1,1,16,27,128,128]{5,4,3,2,1,0:T(8,128)(2,1)S(1)}, bf16[1,1,16,27,128,128]{5,4,3,2,1,0:T(8,128)(2,1)}, u32[]{:S(2)}) copy-start(bf16[1,1,16,27,128,128]{5,4,3,2,1,0:T(8,128)(2,1)} %param.6) | copy-start | bytes 42467332
  51.1 1.0 copy-start.2
  52.2 0.7 copy-start.3
  52.9 0.7 copy-start.4
  67.0 3.2 %copy-start = (bf16[32,8,128,128]{3,2,1,0:T(8,128)(2,1)}, bf16[32,8,128,128]{3,2,1,0:T(8,128)(2,1)S(1)}, u32[]{:S(2)}) copy-start(bf16[32,8,128,128]{3,2,1,0:T(8,128)(2,1)S(1)} %shard_map.64) | copy-start | bytes 25165828
  70.2 185.1 %all-to-all-start.1 = ((bf16[32,8,128,128]{3,2,1,0:T(8,128)(2,1)}), bf16[32,8,128,128]{3,2,1,0:T(8,128)(2,1)}, u32[]{:S(2)}, u32[]{:S(2)}) async-start(bf16[32,8,128,128]{3,2,1,0:T(8,128)(2,1)} %copy-done), calls=%async_computation.1 | async-start | bytes 16777216 | tf_op jit(solution)/shard_map/all_to_all | solution.py:182

commit v2 on v1

--- a/solution.py
+++ b/solution.py
@@ -1,4 +1,5 @@
 import functools
+import math
 
 import jax
 import jax.numpy as jnp
@@ -87,7 +88,7 @@
                 pltpu.SemaphoreType.DMA((9,)),
             ],
         ),
-        compiler_params=pltpu.CompilerParams(vmem_limit_bytes=24 << 20),
+        compiler_params=pltpu.CompilerParams(vmem_limit_bytes=60 << 20),
         cost_estimate=pl.CostEstimate(
             flops=flops, bytes_accessed=2 * steps * (tiles + touched) * size**2, transcendentals=0
         ),
@@ -102,27 +103,32 @@
     def _():
         out_ref[...] = rest[0][...] if carried else jnp.zeros_like(out_ref)
 
-    @pl.when(valid[step] > 0)
-    def _():
-        for f in range(recv_ref.shape[1]):
-            out_ref[segment[step, f]] += recv_ref[0, f].astype(jnp.float32)
+    batch = recv_ref.shape[0]
+    for j in range(batch):
+        slot = step * batch + j
+
+        @pl.when(valid[slot] > 0)
+        def _():
+            for f in range(recv_ref.shape[1]):
+                out_ref[segment[slot, f]] += recv_ref[j, f].astype(jnp.float32)
 
 
 def coarse_sums(recv, segment, valid, total, previous):
     slot_total, touched, size, _ = recv.shape
     whole = pl.BlockSpec((total, size, size), lambda i, *_: (0, 0, 0), pipeline_mode=pl.Buffered(1))
     carried = previous is not None
+    batch = math.gcd(slot_total, 4)
     return pl.pallas_call(
         functools.partial(sum_kernel, carried),
         out_shape=jax.ShapeDtypeStruct((total, size, size), jnp.float32),
         grid_spec=pltpu.PrefetchScalarGridSpec(
             num_scalar_prefetch=2,
-            grid=(slot_total,),
-            in_specs=[pl.BlockSpec((1, touched, size, size), lambda i, *_: (i, 0, 0, 0))]
+            grid=(slot_total // batch,),
+            in_specs=[pl.BlockSpec((batch, touched, size, size), lambda i, *_: (i, 0, 0, 0))]
             + [whole] * carried,
             out_specs=pl.BlockSpec((total, size, size), lambda i, *_: (0, 0, 0)),
         ),
-        compiler_params=pltpu.CompilerParams(vmem_limit_bytes=32 << 20),
+        compiler_params=pltpu.CompilerParams(vmem_limit_bytes=60 << 20),
         cost_estimate=pl.CostEstimate(
             flops=slot_total * touched * size**2,
             bytes_accessed=(2 * slot_total * touched + 4 * total) * size**2,

time: 280 us -> 269 us (0.961)
  local copies, waits for them, and re-layouts: 11.5 us -> 2.04 us
    unnamed x10 -> x12, local copies, waits for them, and re-layouts: 10.7 us -> 0.02 us
    pallas_call x1, Pallas kernels: 20.2 us -> 10.3 us  [coarse_sums(): pl.pallas_call(functools.partial(sum_kernel, carried), out_shape=jax.Shap...]
    pallas_call x1, Pallas kernels: 13.4 us -> 21.2 us  [row_products(): pl.pallas_call(row_kernel, out_shape=jax.ShapeDtypeStruct((slot_total, to...]
  transfers between devices with their start and end apart: 10 -> 10, of which waited for: 3 -> 3; matrix products, arithmetic and copies ran while one was open for 1% -> 2% of each run, Pallas kernels for 5% -> 8%
where the time goes in v2:
time: 269 us; the launch traced here: 264 us
  waiting for transfers between devices  191 us (71%)
  starting transfers between devices  35.4 us (13%)
  Pallas kernels  31.6 us (12%)
  other arithmetic  3.24 us (1%)
    all_to_all x1, waiting for transfers between devices, shards(): lax.all_to_all(s, 'gy', split_axis=0, concat_axis=0, tiled=True)  180 us
    ppermute x8, starting transfers between devices, shifted(): return lax.ppermute(block, axis, pairs)  24.4 us
    pallas_call x1, Pallas kernels, row_products(): pl.pallas_call(row_kernel, out_shape=jax.ShapeDtypeStruct((slot_total, to...  21.2 us
    ppermute x8, waiting for transfers between devices, shifted(): return lax.ppermute(block, axis, pairs)  11.5 us
    pallas_call x1, Pallas kernels, coarse_sums(): pl.pallas_call(functools.partial(sum_kernel, carried), out_shape=jax.Shap...  10.3 us
    all_to_all x1, starting transfers between devices, shards(): lax.all_to_all(meta_sent, 'gy', split_axis=1, concat_axis=1, tiled=True)  5.56 us
    all_to_all x1, starting transfers between devices, shards(): lax.all_to_all(s, 'gy', split_axis=0, concat_axis=0, tiled=True)  5.46 us
  transfers between devices with their start and end apart: 10, of which 3 were waited for; matrix products, arithmetic and copies ran while one was open for 2% of the time, Pallas kernels for 8%

profile of v2, /device:TPU:9, one launch (start us, length us, event | category | flops | bytes accessed | tf_op | source)
XLA Modules:
  0.0 264.5 jit_solution(6739815098481322981)
XLA Ops:
  0.0 3.1 %collective-permute-start = (bf16[16,128,128]{2,1,0:T(8,128)(2,1)}, bf16[16,128,128]{2,1,0:T(8,128)(2,1)S(1)}, u32[]{:S(2)}, u32[]{:S(2)}) collective-permute-start(bf16[16,128,128]{2,1,0:T(8,128)(2,1)} %bitcast.30), channel_id=1, source_target_pairs={{0,1},{1,2},{2,3},{3,4},{4,5},{5,6},{6,7},{8,9},{9,10},{10,11},{11... | collective-permute-start | bytes 1572872 | tf_op jit(solution)/shard_map/ppermute | solution.py:19
  3.1 3.1 %collective-permute-start.3 = (bf16[16,128,128]{2,1,0:T(8,128)(2,1)}, bf16[16,128,128]{2,1,0:T(8,128)(2,1)S(1)}, u32[]{:S(2)}, u32[]{:S(2)}) collective-permute-start(bf16[16,128,128]{2,1,0:T(8,128)(2,1)} %bitcast.31), channel_id=1, source_target_pairs={{1,0},{2,1},{3,2},{4,3},{5,4},{6,5},{7,6},{9,8},{10,9},{11,10},{12... | collective-permute-start | bytes 1572872 | tf_op jit(solution)/shard_map/ppermute | solution.py:19
  6.2 4.3 %collective-permute-start.2 = (bf16[16,128,128]{2,1,0:T(8,128)(2,1)}, bf16[16,128,128]{2,1,0:T(8,128)(2,1)S(1)}, u32[]{:S(2)}, u32[]{:S(2)}) collective-permute-start(bf16[16,128,128]{2,1,0:T(8,128)(2,1)} %bitcast.32), channel_id=1, source_target_pairs={{0,8},{8,16},{16,24},{1,9},{9,17},{17,25},{2,10},{10,18},{18,26},{... | collective-permute-start | bytes 1572872 | tf_op jit(solution)/shard_map/ppermute | solution.py:19
  10.5 1.9 collective-permute-start.6
  12.4 0.7 and_select_fusion.3
  13.1 0.2 convert_reduce_fusion.1
  13.2 0.7 bitcast_add_fusion
  13.9 0.7 convert_reduce_fusion.2
  15.3 0.1 iota_compare_fusion.1
  15.3 9.9 %collective-permute-done.rest_3_ = bf16[16,128,128]{2,1,0:T(8,128)(2,1)S(1)} collective-permute-done((bf16[16,128,128]{2,1,0:T(8,128)(2,1)}, bf16[16,128,128]{2,1,0:T(8,128)(2,1)S(1)}, u32[]{:S(2)}, u32[]{:S(2)}) %collective-permute-start) | collective-permute-done | bytes 524320 | tf_op jit(solution)/shard_map/ppermute | solution.py:19
  25.3 0.0 copy-start
  25.3 4.6 %collective-permute-start.1 = (bf16[16,128,128]{2,1,0:T(8,128)(2,1)S(1)}, bf16[16,128,128]{2,1,0:T(8,128)(2,1)S(1)}, u32[]{:S(2)}, u32[]{:S(2)}) collective-permute-start(bf16[16,128,128]{2,1,0:T(8,128)(2,1)S(1)} %collective-permute-done.rest_3_), channel_id=1, source_target_pairs={{0,8},{8,16},{16,24},{1,9},{9,17},{17,25},{2,10},{10,18},{18,26},{... | collective-permute-start | bytes 1572872 | tf_op jit(solution)/shard_map/ppermute | solution.py:19
  29.8 1.9 collective-permute-start.5
  31.7 0.0 collective-permute-done.3.rest_5_
  31.8 0.0 copy-start.1
  31.8 3.6 %collective-permute-start.4 = (bf16[16,128,128]{2,1,0:T(8,128)(2,1)S(1)}, bf16[16,128,128]{2,1,0:T(8,128)(2,1)}, u32[]{:S(2)}, u32[]{:S(2)}) collective-permute-start(bf16[16,128,128]{2,1,0:T(8,128)(2,1)S(1)} %collective-permute-done.3.rest_5_), channel_id=1, source_target_pairs={{0,8},{8,16},{16,24},{1,9},{9,17},{17,25},{2,10},{10,18},{18,26},{... | collective-permute-start | bytes 1572872 | tf_op jit(solution)/shard_map/ppermute | solution.py:19
  35.4 0.0 collective-permute-done.2.rest_1_
  35.4 0.0 copy-start.2
  35.4 1.9 collective-permute-start.7
  37.4 0.1 select_reduce_fusion
  37.5 0.7 copy.11
  38.2 5.6 %all-to-all-start = ((s32[1,8,4,9]{3,2,0,1:T(4,128)}), s32[1,8,4,9]{3,2,0,1:T(4,128)S(1)}, u32[]{:S(2)}, u32[]{:S(2)}) async-start(s32[1,8,4,9]{3,2,0,1:T(4,128)} %bitcast.3), calls=%async_computation | async-start | bytes 32768 | tf_op jit(solution)/shard_map/all_to_all | solution.py:167
  43.7 0.1 convert_reduce_fusion
  43.8 0.7 select_reduce_fusion.1
  44.6 0.0 collective-permute-done.6.rest_7_
  44.6 0.0 copy-start.3
  44.6 0.0 collective-permute-done.1.rest_0_
  44.6 0.0 copy-start.4
  44.6 0.0 collective-permute-done.4.rest_2_
  44.6 0.0 collective-permute-done.5.rest_6_
  44.6 0.0 copy-start.5
  44.6 1.5 collective-permute-done.7.rest_8_
  46.2 0.0 copy-done
  46.2 0.0 copy-done.1
  46.2 0.0 copy-done.2
  46.2 0.0 copy-done.3
  46.2 0.0 copy-done.4
  46.2 0.0 copy-done.5
  46.2 21.2 %shard_map.64 = bf16[32,8,128,128]{3,2,1,0:T(8,128)(2,1)} custom-call(s32[16]{0:T(128)} %get-tuple-element.6.order, s32[16]{0:T(128)} %get-tuple-element.5.place, s32[1]{0:T(128)} %bitcast.6.count, s32[16,27]{1,0:T(8,128)} %bitcast.37, s32[16,27]{1,0:T(8,128)} %bitcast.38, bf16[16,27,128,128]{3,2,1,0:T(8,128)(2,1)} %bitcast.29, ...), custom_call_target="tpu_custom_call" | custom-call | flops 2348810240 | bytes 18350080 | tf_op jit(solution)/shard_map/pallas_call | solution.py:70
  67.4 0.0 all-to-all-done
  67.4 5.5 %all-to-all-start.1 = ((bf16[32,8,128,128]{3,2,1,0:T(8,128)(2,1)}), bf16[32,8,128,128]{3,2,1,0:T(8,128)(2,1)}, u32[]{:S(2)}, u32[]{:S(2)}) async-start(bf16[32,8,128,128]{3,2,1,0:T(8,128)(2,1)} %shard_map.64), calls=%async_computation.1 | async-start | bytes 16777216 | tf_op jit(solution)/shard_map/all_to_all | solution.py:188
  72.9 0.7 slice_reduce_fusion.valid
  73.6 0.7 slice_bitcast_fusion.segment
  74.2 179.9 %all-to-all-done.1.recv_ref = bf16[32,8,128,128]{3,2,1,0:T(8,128)(2,1)} async-done(((bf16[32,8,128,128]{3,2,1,0:T(8,128)(2,1)}), bf16[32,8,128,128]{3,2,1,0:T(8,128)(2,1)}, u32[]{:S(2)}, u32[]{:S(2)}) %all-to-all-start.1) | async-done | bytes 8388640 | tf_op jit(solution)/shard_map/all_to_all | solution.py:188
  254.1 10.3 %shard_map.65 = f32[108,128,128]{2,1,0:T(8,128)} custom-call(s32[32,8]{1,0:T(8,128)} %slice_bitcast_fusion.segment, s32[32]{0:T(128)} %slice_reduce_fusion.valid, bf16[32,8,128,128]{3,2,1,0:T(8,128)(2,1)} %all-to-all-done.1.recv_ref), custom_call_target="tpu_custom_call" | custom-call | flops 4194304 | bytes 15466496 | tf_op jit(solution)/shard_map/pallas_call | solution.py:121
  (3 shorter events, 0.0 us)
Async XLA Ops:
  0.0 25.3 %collective-permute-start = (bf16[16,128,128]{2,1,0:T(8,128)(2,1)}, bf16[16,128,128]{2,1,0:T(8,128)(2,1)S(1)}, u32[]{:S(2)}, u32[]{:S(2)}) collective-permute-start(bf16[16,128,128]{2,1,0:T(8,128)(2,1)} %bitcast.30), channel_id=1, source_target_pairs={{0,1},{1,2},{2,3},{3,4},{4,5},{5,6},{6,7},{8,9},{9,10},{10,11},{11... | collective-permute-start | bytes 1572872 | tf_op jit(solution)/shard_map/ppermute | solution.py:19
  3.1 28.6 %collective-permute-start.3 = (bf16[16,128,128]{2,1,0:T(8,128)(2,1)}, bf16[16,128,128]{2,1,0:T(8,128)(2,1)S(1)}, u32[]{:S(2)}, u32[]{:S(2)}) collective-permute-start(bf16[16,128,128]{2,1,0:T(8,128)(2,1)} %bitcast.31), channel_id=1, source_target_pairs={{1,0},{2,1},{3,2},{4,3},{5,4},{6,5},{7,6},{9,8},{10,9},{11,10},{12... | collective-permute-start | bytes 1572872 | tf_op jit(solution)/shard_map/ppermute | solution.py:19
  6.2 29.2 %collective-permute-start.2 = (bf16[16,128,128]{2,1,0:T(8,128)(2,1)}, bf16[16,128,128]{2,1,0:T(8,128)(2,1)S(1)}, u32[]{:S(2)}, u32[]{:S(2)}) collective-permute-start(bf16[16,128,128]{2,1,0:T(8,128)(2,1)} %bitcast.32), channel_id=1, source_target_pairs={{0,8},{8,16},{16,24},{1,9},{9,17},{17,25},{2,10},{10,18},{18,26},{... | collective-permute-start | bytes 1572872 | tf_op jit(solution)/shard_map/ppermute | solution.py:19
  10.5 34.1 %collective-permute-start.6 = (bf16[16,128,128]{2,1,0:T(8,128)(2,1)}, bf16[16,128,128]{2,1,0:T(8,128)(2,1)S(1)}, u32[]{:S(2)}, u32[]{:S(2)}) collective-permute-start(bf16[16,128,128]{2,1,0:T(8,128)(2,1)} %bitcast.33), channel_id=1, source_target_pairs={{8,0},{16,8},{24,16},{9,1},{17,9},{25,17},{10,2},{18,10},{26,18},{... | collective-permute-start | bytes 1572872 | tf_op jit(solution)/shard_map/ppermute | solution.py:19
  25.3 20.9 %copy-start = (bf16[16,128,128]{2,1,0:T(8,128)(2,1)}, bf16[16,128,128]{2,1,0:T(8,128)(2,1)S(1)}, u32[]{:S(2)}) copy-start(bf16[16,128,128]{2,1,0:T(8,128)(2,1)S(1)} %collective-permute-done.rest_3_) | copy-start | bytes 1572868
  25.3 19.3 %collective-permute-start.1 = (bf16[16,128,128]{2,1,0:T(8,128)(2,1)S(1)}, bf16[16,128,128]{2,1,0:T(8,128)(2,1)S(1)}, u32[]{:S(2)}, u32[]{:S(2)}) collective-permute-start(bf16[16,128,128]{2,1,0:T(8,128)(2,1)S(1)} %collective-permute-done.rest_3_), channel_id=1, source_target_pairs={{0,8},{8,16},{16,24},{1,9},{9,17},{17,25},{2,10},{10,18},{18,26},{... | collective-permute-start | bytes 1572872 | tf_op jit(solution)/shard_map/ppermute | solution.py:19
  29.8 14.8 %collective-permute-start.5 = (bf16[16,128,128]{2,1,0:T(8,128)(2,1)S(1)}, bf16[16,128,128]{2,1,0:T(8,128)(2,1)S(1)}, u32[]{:S(2)}, u32[]{:S(2)}) collective-permute-start(bf16[16,128,128]{2,1,0:T(8,128)(2,1)S(1)} %collective-permute-done.rest_3_), channel_id=1, source_target_pairs={{8,0},{16,8},{24,16},{9,1},{17,9},{25,17},{10,2},{18,10},{26,18},{... | collective-permute-start | bytes 1572872 | tf_op jit(solution)/shard_map/ppermute | solution.py:19
  31.8 14.4 %copy-start.1 = (bf16[16,128,128]{2,1,0:T(8,128)(2,1)}, bf16[16,128,128]{2,1,0:T(8,128)(2,1)S(1)}, u32[]{:S(2)}) copy-start(bf16[16,128,128]{2,1,0:T(8,128)(2,1)S(1)} %collective-permute-done.3.rest_5_) | copy-start | bytes 1572868
  31.8 12.8 %collective-permute-start.4 = (bf16[16,128,128]{2,1,0:T(8,128)(2,1)S(1)}, bf16[16,128,128]{2,1,0:T(8,128)(2,1)}, u32[]{:S(2)}, u32[]{:S(2)}) collective-permute-start(bf16[16,128,128]{2,1,0:T(8,128)(2,1)S(1)} %collective-permute-done.3.rest_5_), channel_id=1, source_target_pairs={{0,8},{8,16},{16,24},{1,9},{9,17},{17,25},{2,10},{10,18},{18,26},{... | collective-permute-start | bytes 1572872 | tf_op jit(solution)/shard_map/ppermute | solution.py:19
  35.4 10.8 %copy-start.2 = (bf16[16,128,128]{2,1,0:T(8,128)(2,1)}, bf16[16,128,128]{2,1,0:T(8,128)(2,1)S(1)}, u32[]{:S(2)}) copy-start(bf16[16,128,128]{2,1,0:T(8,128)(2,1)S(1)} %collective-permute-done.2.rest_1_) | copy-start | bytes 1572868
  35.4 10.7 %collective-permute-start.7 = (bf16[16,128,128]{2,1,0:T(8,128)(2,1)S(1)}, bf16[16,128,128]{2,1,0:T(8,128)(2,1)}, u32[]{:S(2)}, u32[]{:S(2)}) collective-permute-start(bf16[16,128,128]{2,1,0:T(8,128)(2,1)S(1)} %collective-permute-done.3.rest_5_), channel_id=1, source_target_pairs={{8,0},{16,8},{24,16},{9,1},{17,9},{25,17},{10,2},{18,10},{26,18},{... | collective-permute-start | bytes 1572872 | tf_op jit(solution)/shard_map/ppermute | solution.py:19
  38.2 29.3 %all-to-all-start = ((s32[1,8,4,9]{3,2,0,1:T(4,128)}), s32[1,8,4,9]{3,2,0,1:T(4,128)S(1)}, u32[]{:S(2)}, u32[]{:S(2)}) async-start(s32[1,8,4,9]{3,2,0,1:T(4,128)} %bitcast.3), calls=%async_computation | async-start | bytes 32768 | tf_op jit(solution)/shard_map/all_to_all | solution.py:167
  44.6 1.6 copy-start.3
  44.6 1.6 copy-start.4
  44.6 1.6 copy-start.5
  67.4 186.7 %all-to-all-start.1 = ((bf16[32,8,128,128]{3,2,1,0:T(8,128)(2,1)}), bf16[32,8,128,128]{3,2,1,0:T(8,128)(2,1)}, u32[]{:S(2)}, u32[]{:S(2)}) async-start(bf16[32,8,128,128]{3,2,1,0:T(8,128)(2,1)} %shard_map.64), calls=%async_computation.1 | async-start | bytes 16777216 | tf_op jit(solution)/shard_map/all_to_all | solution.py:188

commit v3 on v2

--- a/solution.py
+++ b/solution.py
@@ -10,7 +10,7 @@
 
 KC = 27
 AGG = 4
-CHUNKS = 1
+MESH = pl.DeviceIdType.MESH
 
 
 def shifted(block, axis, step):
@@ -95,13 +95,12 @@
     )(order, place, count, near, group, a_local, *pieces)
 
 
-def sum_kernel(carried, segment, valid, recv_ref, *rest):
-    out_ref = rest[-1]
+def sum_kernel(segment, valid, recv_ref, out_ref):
     step = pl.program_id(0)
 
     @pl.when(step == 0)
     def _():
-        out_ref[...] = rest[0][...] if carried else jnp.zeros_like(out_ref)
+        out_ref[...] = jnp.zeros_like(out_ref)
 
     batch = recv_ref.shape[0]
     for j in range(batch):
@@ -113,19 +112,16 @@
                 out_ref[segment[slot, f]] += recv_ref[j, f].astype(jnp.float32)
 
 
-def coarse_sums(recv, segment, valid, total, previous):
+def coarse_sums(recv, segment, valid, total):
     slot_total, touched, size, _ = recv.shape
-    whole = pl.BlockSpec((total, size, size), lambda i, *_: (0, 0, 0), pipeline_mode=pl.Buffered(1))
-    carried = previous is not None
     batch = math.gcd(slot_total, 4)
     return pl.pallas_call(
-        functools.partial(sum_kernel, carried),
+        sum_kernel,
         out_shape=jax.ShapeDtypeStruct((total, size, size), jnp.float32),
         grid_spec=pltpu.PrefetchScalarGridSpec(
             num_scalar_prefetch=2,
             grid=(slot_total // batch,),
-            in_specs=[pl.BlockSpec((batch, touched, size, size), lambda i, *_: (i, 0, 0, 0))]
-            + [whole] * carried,
+            in_specs=[pl.BlockSpec((batch, touched, size, size), lambda i, *_: (i, 0, 0, 0))],
             out_specs=pl.BlockSpec((total, size, size), lambda i, *_: (0, 0, 0)),
         ),
         compiler_params=pltpu.CompilerParams(vmem_limit_bytes=60 << 20),
@@ -134,7 +130,73 @@
             bytes_accessed=(2 * slot_total * touched + 4 * total) * size**2,
             transcendentals=0,
         ),
-    )(segment, valid, recv, *([previous] if carried else []))
+    )(segment, valid, recv)
+
+
+def partner(me, bits, count):
+    if count & (count - 1):
+        return (me + bits) % count
+    target, unit = 0, 1
+    while unit < count:
+        bit = me // unit % 2
+        target = target + unit * (1 - bit if bits & unit else bit)
+        unit *= 2
+    return target
+
+
+def swap_kernel(count, width, sent, meta, recv, meta_recv, send_sems, recv_sems, local_sems):
+    me = lax.axis_index("gy")
+    block = lambda owner: pl.ds(owner * width, width)
+    barrier = pltpu.get_barrier_semaphore()
+    for bits in range(1, count):
+        pl.semaphore_signal(
+            barrier, inc=1, device_id={"gy": partner(me, bits, count)}, device_id_type=MESH
+        )
+    pl.semaphore_wait(barrier, count - 1)
+    copies = []
+    for bits in range(1, count):
+        target = partner(me, bits, count)
+        for j, (source, place) in enumerate(
+            ((meta.at[target], meta_recv.at[me]), (sent.at[block(target)], recv.at[block(me)]))
+        ):
+            copies.append(
+                pltpu.make_async_remote_copy(
+                    src_ref=source,
+                    dst_ref=place,
+                    send_sem=send_sems.at[j, bits - 1],
+                    recv_sem=recv_sems.at[j, bits - 1],
+                    device_id={"gy": target},
+                    device_id_type=MESH,
+                )
+            )
+    copies.append(pltpu.make_async_copy(meta.at[me], meta_recv.at[me], local_sems.at[0]))
+    copies.append(
+        pltpu.make_async_copy(sent.at[block(me)], recv.at[block(me)], local_sems.at[1])
+    )
+    for copy in copies:
+        copy.start()
+    for copy in copies:
+        copy.wait()
+
+
+def swapped(sent, meta, count, width):
+    return pl.pallas_call(
+        functools.partial(swap_kernel, count, width),
+        out_shape=(
+            jax.ShapeDtypeStruct(sent.shape, sent.dtype),
+            jax.ShapeDtypeStruct(meta.shape, meta.dtype),
+        ),
+        in_specs=[pl.BlockSpec(memory_space=pl.ANY)] * 2,
+        out_specs=[pl.BlockSpec(memory_space=pl.ANY)] * 2,
+        scratch_shapes=[
+            pltpu.SemaphoreType.DMA((2, count - 1)),
+            pltpu.SemaphoreType.DMA((2, count - 1)),
+            pltpu.SemaphoreType.DMA((2,)),
+        ],
+        compiler_params=pltpu.CompilerParams(
+            collective_id=0, has_side_effects=True, vmem_limit_bytes=60 << 20
+        ),
+    )(sent, meta)
 
 
 def shards(a_tiles, p_tiles, neighbours, groups, slots, aggregates):
@@ -155,41 +217,22 @@
     same_owner = owners[:, None] == owners[None, :]
     earlier = indices[:, None] > indices[None, :]
     rank = jnp.sum((same_owner & earlier).astype(jnp.int32), axis=1)
-    chunks = min(CHUNKS, row_cap)
-    width = row_cap // chunks
-    position = (rank // width * owner_count + owners) * width + rank % width
+    position = owners * row_cap + rank
     slot_total = owner_count * row_cap
     selector = jnp.arange(slot_total, dtype=jnp.int32)[:, None] == position[None, :]
     segments = local_row[:, None] * KC + slot_local
     meta = jnp.concatenate([jnp.ones_like(local_row)[:, None], segments], axis=1)
     meta_sent = jnp.sum(jnp.where(selector[:, :, None], meta[None], 0), axis=1)
-    meta_sent = meta_sent.reshape(chunks, owner_count, width, touched + 1)
-    meta_recv = lax.all_to_all(meta_sent, "gy", split_axis=1, concat_axis=1, tiled=True)
-    meta_recv = meta_recv.reshape(chunks, owner_count * width, touched + 1)
-
-    pieces = halo(p_local)
-    coarse = None
-    sent = []
-    for chunk in range(chunks):
-        steps = min(row_count, owner_count * width, row_count)
-        active = rank // width == chunk
-        count = jnp.sum(active.astype(jnp.int32))
-        ahead = jnp.sum((active[None, :] & earlier).astype(jnp.int32), axis=1)
-        wanted = jnp.minimum(jnp.arange(steps, dtype=jnp.int32), count - 1)
-        chosen = active[None, :] & (ahead[None, :] == wanted[:, None])
-        order = jnp.sum(jnp.where(chosen, indices[None, :], 0), axis=1)
-        place = jnp.sum(jnp.where(chosen, (owners * width + rank % width)[None, :], 0), axis=1)
-        sent.append(
-            row_products(
-                a_local, pieces, near, group, order, place, count[None],
-                owner_count * width, touched,
-            )
-        )
-    recv = [lax.all_to_all(s, "gy", split_axis=0, concat_axis=0, tiled=True) for s in sent]
-    for chunk in range(chunks):
-        coarse = coarse_sums(
-            recv[chunk], meta_recv[chunk, :, 1:], meta_recv[chunk, :, 0], total, coarse
-        )
+    meta_sent = meta_sent.reshape(owner_count, row_cap, touched + 1)
+    meta_sent = jnp.pad(meta_sent, ((0, 0), (0, -row_cap % 8), (0, -(touched + 1) % 128)))
+
+    sent = row_products(
+        a_local, halo(p_local), near, group, indices, position,
+        jnp.full((1,), row_count, jnp.int32), slot_total, touched,
+    )
+    recv, meta_recv = swapped(sent, meta_sent, owner_count, row_cap)
+    meta_recv = meta_recv[:, :row_cap, : touched + 1].reshape(slot_total, touched + 1)
+    coarse = coarse_sums(recv, meta_recv[:, 1:], meta_recv[:, 0], total)
     return coarse.reshape(1, 1, coarse_rows, KC, size, size)
 
 

time: 269 us -> 263 us (0.978); the launches traced: 264 us -> 262 us
  Pallas kernels: 31.6 us -> 212 us
  waiting for transfers between devices: 191 us -> 22 us
  starting transfers between devices: 35.4 us -> 22.4 us
    pallas_call x1 -> x2, Pallas kernels: 10.3 us -> 191 us  [the longest x1 181 us: swapped(): pl.pallas_call(functools.partial(swap_kernel, count, width), out_shape=(j...]
    all_to_all x2 -> x0, waiting for transfers between devices: 180 us -> none  [the longest x1 180 us: shards(): lax.all_to_all(s, 'gy', split_axis=0, concat_axis=0, tiled=True)]
    all_to_all x2 -> x0, starting transfers between devices: 11 us -> none  [the longest x1 5.56 us: shards(): lax.all_to_all(meta_sent, 'gy', split_axis=1, concat_axis=1, tiled=True)]
    ppermute x8, waiting for transfers between devices: 11.5 us -> 22 us  [shifted(): return lax.ppermute(block, axis, pairs)]
  transfers between devices with their start and end apart: 10 -> 8, of which waited for: 3 -> 3; matrix products, arithmetic and copies ran while one was open for 2% -> 1% of each run, Pallas kernels for 8% -> 0%
where the time goes in v3:
time: 263 us; the launch traced here: 262 us
  Pallas kernels  212 us (81%)
  starting transfers between devices  22.4 us (9%)
  waiting for transfers between devices  22 us (8%)
  local copies, waits for them, and re-layouts  3.42 us (1%)
    pallas_call x1, Pallas kernels, swapped(): pl.pallas_call(functools.partial(swap_kernel, count, width), out_shape=(j...  181 us
    ppermute x8, starting transfers between devices, shifted(): return lax.ppermute(block, axis, pairs)  22.4 us
    ppermute x8, waiting for transfers between devices, shifted(): return lax.ppermute(block, axis, pairs)  22 us
    pallas_call x1, Pallas kernels, row_products(): pl.pallas_call(row_kernel, out_shape=jax.ShapeDtypeStruct((slot_total, to...  20.6 us
    pallas_call x1, Pallas kernels, coarse_sums(): pl.pallas_call(sum_kernel, out_shape=jax.ShapeDtypeStruct((total, size, s...  10.3 us
  transfers between devices with their start and end apart: 8, of which 3 were waited for; matrix products, arithmetic and copies ran while one was open for 1% of the time, Pallas kernels for 0%

profile of v3, /device:TPU:9, one launch (start us, length us, event | category | flops | bytes accessed | tf_op | source)
XLA Modules:
  0.0 261.6 jit_solution(8224018234792511089)
XLA Ops:
  0.0 2.6 collective-permute-start.6
  2.6 3.0 %collective-permute-start.3 = (bf16[16,128,128]{2,1,0:T(8,128)(2,1)}, bf16[16,128,128]{2,1,0:T(8,128)(2,1)S(1)}, u32[]{:S(2)}, u32[]{:S(2)}) collective-permute-start(bf16[16,128,128]{2,1,0:T(8,128)(2,1)} %bitcast.26), channel_id=1, source_target_pairs={{1,0},{2,1},{3,2},{4,3},{5,4},{6,5},{7,6},{9,8},{10,9},{11,10},{12... | collective-permute-start | bytes 1572872 | tf_op jit(solution)/shard_map/ppermute | solution.py:19
  5.6 3.3 %collective-permute-start.2 = (bf16[16,128,128]{2,1,0:T(8,128)(2,1)}, bf16[16,128,128]{2,1,0:T(8,128)(2,1)S(1)}, u32[]{:S(2)}, u32[]{:S(2)}) collective-permute-start(bf16[16,128,128]{2,1,0:T(8,128)(2,1)} %bitcast.27), channel_id=1, source_target_pairs={{0,8},{8,16},{16,24},{1,9},{9,17},{17,25},{2,10},{10,18},{18,26},{... | collective-permute-start | bytes 1572872 | tf_op jit(solution)/shard_map/ppermute | solution.py:19
  8.9 2.3 collective-permute-start
  11.2 0.7 fusion.1
  11.9 0.7 bitcast_add_fusion
  12.6 0.2 convert_reduce_fusion
  12.8 16.8 %collective-permute-done.3.rest_5_ = bf16[16,128,128]{2,1,0:T(8,128)(2,1)S(1)} collective-permute-done((bf16[16,128,128]{2,1,0:T(8,128)(2,1)}, bf16[16,128,128]{2,1,0:T(8,128)(2,1)S(1)}, u32[]{:S(2)}, u32[]{:S(2)}) %collective-permute-start.3) | collective-permute-done | bytes 524320 | tf_op jit(solution)/shard_map/ppermute | solution.py:19
  29.6 0.0 copy-start.1
  29.6 2.3 collective-permute-start.7
  31.9 3.4 %collective-permute-start.4 = (bf16[16,128,128]{2,1,0:T(8,128)(2,1)S(1)}, bf16[16,128,128]{2,1,0:T(8,128)(2,1)S(1)}, u32[]{:S(2)}, u32[]{:S(2)}) collective-permute-start(bf16[16,128,128]{2,1,0:T(8,128)(2,1)S(1)} %collective-permute-done.3.rest_5_), channel_id=1, source_target_pairs={{0,8},{8,16},{16,24},{1,9},{9,17},{17,25},{2,10},{10,18},{18,26},{... | collective-permute-start | bytes 1572872 | tf_op jit(solution)/shard_map/ppermute | solution.py:19
  35.3 0.0 collective-permute-done.rest_3_
  35.3 0.0 copy-start.3
  35.3 1.9 collective-permute-start.5
  37.2 0.0 collective-permute-done.6.rest_7_
  37.2 0.0 copy-start
  37.2 3.6 %collective-permute-start.1 = (bf16[16,128,128]{2,1,0:T(8,128)(2,1)S(1)}, bf16[16,128,128]{2,1,0:T(8,128)(2,1)}, u32[]{:S(2)}, u32[]{:S(2)}) collective-permute-start(bf16[16,128,128]{2,1,0:T(8,128)(2,1)S(1)} %collective-permute-done.rest_3_), channel_id=1, source_target_pairs={{0,8},{8,16},{16,24},{1,9},{9,17},{17,25},{2,10},{10,18},{18,26},{... | collective-permute-start | bytes 1572872 | tf_op jit(solution)/shard_map/ppermute | solution.py:19
  40.9 0.0 copy-start.6
  40.9 0.1 iota_compare_fusion
  41.0 0.1 select_reduce_fusion
  41.1 0.1 copy.9
  41.2 0.6 pad.5.meta
  41.8 0.0 collective-permute-done.2.rest_1_
  41.8 0.0 copy-start.2
  41.8 0.0 collective-permute-done.7.rest_8_
  41.8 0.0 copy-start.4
  41.8 0.0 collective-permute-done.4.rest_2_
  41.8 0.0 copy-start.5
  41.8 4.1 %collective-permute-done.5.rest_6_ = bf16[16,128,128]{2,1,0:T(8,128)(2,1)} collective-permute-done((bf16[16,128,128]{2,1,0:T(8,128)(2,1)S(1)}, bf16[16,128,128]{2,1,0:T(8,128)(2,1)}, u32[]{:S(2)}, u32[]{:S(2)}) %collective-permute-start.5) | collective-permute-done | bytes 524320 | tf_op jit(solution)/shard_map/ppermute | solution.py:19
  45.9 1.1 collective-permute-done.1.rest_0_
  47.0 0.6 iota.17.order
  47.6 0.0 copy-done.1
  47.6 0.0 copy-done.3
  47.6 0.0 copy-done
  47.6 0.0 copy-done.6
  47.6 0.0 copy-done.2
  47.6 0.0 copy-done.4
  47.6 0.0 copy-done.5
  47.6 20.6 %shard_map.64.sent = bf16[32,8,128,128]{3,2,1,0:T(8,128)(2,1)} custom-call(s32[16]{0:T(128)} %iota.17.order, s32[16]{0:T(128)} %copy-done.6, s32[1]{0:T(128)} %constant.33.clone.1.count, s32[16,27]{1,0:T(8,128)} %bitcast.33, s32[16,27]{1,0:T(8,128)} %bitcast.34, bf16[16,27,128,128]{3,2,1,0:T(8,128)(2,1)} %bitcast.24, ...), custom_call_target="tpu_custom_call" | custom-call | flops 2348810240 | bytes 18350080 | tf_op jit(solution)/shard_map/pallas_call | solution.py:70
  68.2 181.0 %shard_map.65 = (bf16[32,8,128,128]{3,2,1,0:T(8,128)(2,1)}, s32[8,8,128]{2,1,0:T(8,128)}) custom-call(bf16[32,8,128,128]{3,2,1,0:T(8,128)(2,1)} %shard_map.64.sent, s32[8,8,128]{2,1,0:T(8,128)} %pad.5.meta), custom_call_target="tpu_custom_call" | custom-call | tf_op jit(solution)/shard_map/pallas_call | solution.py:183
  249.2 0.8 slice.9
  249.9 0.7 slice_reduce_fusion.valid
  250.6 0.7 slice.12.segment
  251.3 10.3 %shard_map.66 = f32[108,128,128]{2,1,0:T(8,128)} custom-call(s32[32,8]{1,0:T(8,128)} %slice.12.segment, s32[32]{0:T(128)} %slice_reduce_fusion.valid, bf16[32,8,128,128]{3,2,1,0:T(8,128)(2,1)} %get-tuple-element.8.recv_ref), custom_call_target="tpu_custom_call" | custom-call | flops 4194304 | bytes 15466496 | tf_op jit(solution)/shard_map/pallas_call | solution.py:118
  (2 shorter events, 0.0 us)
Async XLA Ops:
  0.0 37.2 %collective-permute-start.6 = (bf16[16,128,128]{2,1,0:T(8,128)(2,1)}, bf16[16,128,128]{2,1,0:T(8,128)(2,1)S(1)}, u32[]{:S(2)}, u32[]{:S(2)}) collective-permute-start(bf16[16,128,128]{2,1,0:T(8,128)(2,1)} %bitcast.25), channel_id=1, source_target_pairs={{8,0},{16,8},{24,16},{9,1},{17,9},{25,17},{10,2},{18,10},{26,18},{... | collective-permute-start | bytes 1572872 | tf_op jit(solution)/shard_map/ppermute | solution.py:19
  2.6 27.0 %collective-permute-start.3 = (bf16[16,128,128]{2,1,0:T(8,128)(2,1)}, bf16[16,128,128]{2,1,0:T(8,128)(2,1)S(1)}, u32[]{:S(2)}, u32[]{:S(2)}) collective-permute-start(bf16[16,128,128]{2,1,0:T(8,128)(2,1)} %bitcast.26), channel_id=1, source_target_pairs={{1,0},{2,1},{3,2},{4,3},{5,4},{6,5},{7,6},{9,8},{10,9},{11,10},{12... | collective-permute-start | bytes 1572872 | tf_op jit(solution)/shard_map/ppermute | solution.py:19
  5.6 36.2 %collective-permute-start.2 = (bf16[16,128,128]{2,1,0:T(8,128)(2,1)}, bf16[16,128,128]{2,1,0:T(8,128)(2,1)S(1)}, u32[]{:S(2)}, u32[]{:S(2)}) collective-permute-start(bf16[16,128,128]{2,1,0:T(8,128)(2,1)} %bitcast.27), channel_id=1, source_target_pairs={{0,8},{8,16},{16,24},{1,9},{9,17},{17,25},{2,10},{10,18},{18,26},{... | collective-permute-start | bytes 1572872 | tf_op jit(solution)/shard_map/ppermute | solution.py:19
  8.9 26.3 %collective-permute-start = (bf16[16,128,128]{2,1,0:T(8,128)(2,1)}, bf16[16,128,128]{2,1,0:T(8,128)(2,1)S(1)}, u32[]{:S(2)}, u32[]{:S(2)}) collective-permute-start(bf16[16,128,128]{2,1,0:T(8,128)(2,1)} %bitcast.28), channel_id=1, source_target_pairs={{0,1},{1,2},{2,3},{3,4},{4,5},{5,6},{6,7},{8,9},{9,10},{10,11},{11... | collective-permute-start | bytes 1572872 | tf_op jit(solution)/shard_map/ppermute | solution.py:19
  29.6 18.0 %copy-start.1 = (bf16[16,128,128]{2,1,0:T(8,128)(2,1)}, bf16[16,128,128]{2,1,0:T(8,128)(2,1)S(1)}, u32[]{:S(2)}) copy-start(bf16[16,128,128]{2,1,0:T(8,128)(2,1)S(1)} %collective-permute-done.3.rest_5_) | copy-start | bytes 1572868
  29.6 12.2 %collective-permute-start.7 = (bf16[16,128,128]{2,1,0:T(8,128)(2,1)S(1)}, bf16[16,128,128]{2,1,0:T(8,128)(2,1)S(1)}, u32[]{:S(2)}, u32[]{:S(2)}) collective-permute-start(bf16[16,128,128]{2,1,0:T(8,128)(2,1)S(1)} %collective-permute-done.3.rest_5_), channel_id=1, source_target_pairs={{8,0},{16,8},{24,16},{9,1},{17,9},{25,17},{10,2},{18,10},{26,18},{... | collective-permute-start | bytes 1572872 | tf_op jit(solution)/shard_map/ppermute | solution.py:19
  31.9 9.9 %collective-permute-start.4 = (bf16[16,128,128]{2,1,0:T(8,128)(2,1)S(1)}, bf16[16,128,128]{2,1,0:T(8,128)(2,1)S(1)}, u32[]{:S(2)}, u32[]{:S(2)}) collective-permute-start(bf16[16,128,128]{2,1,0:T(8,128)(2,1)S(1)} %collective-permute-done.3.rest_5_), channel_id=1, source_target_pairs={{0,8},{8,16},{16,24},{1,9},{9,17},{17,25},{2,10},{10,18},{18,26},{... | collective-permute-start | bytes 1572872 | tf_op jit(solution)/shard_map/ppermute | solution.py:19
  35.3 12.3 %copy-start.3 = (bf16[16,128,128]{2,1,0:T(8,128)(2,1)}, bf16[16,128,128]{2,1,0:T(8,128)(2,1)S(1)}, u32[]{:S(2)}) copy-start(bf16[16,128,128]{2,1,0:T(8,128)(2,1)S(1)} %collective-permute-done.rest_3_) | copy-start | bytes 1572868
  35.3 10.6 %collective-permute-start.5 = (bf16[16,128,128]{2,1,0:T(8,128)(2,1)S(1)}, bf16[16,128,128]{2,1,0:T(8,128)(2,1)}, u32[]{:S(2)}, u32[]{:S(2)}) collective-permute-start(bf16[16,128,128]{2,1,0:T(8,128)(2,1)S(1)} %collective-permute-done.rest_3_), channel_id=1, source_target_pairs={{8,0},{16,8},{24,16},{9,1},{17,9},{25,17},{10,2},{18,10},{26,18},{... | collective-permute-start | bytes 1572872 | tf_op jit(solution)/shard_map/ppermute | solution.py:19
  37.2 10.3 %copy-start = (bf16[16,128,128]{2,1,0:T(8,128)(2,1)}, bf16[16,128,128]{2,1,0:T(8,128)(2,1)S(1)}, u32[]{:S(2)}) copy-start(bf16[16,128,128]{2,1,0:T(8,128)(2,1)S(1)} %collective-permute-done.6.rest_7_) | copy-start | bytes 1572868
  37.2 9.8 %collective-permute-start.1 = (bf16[16,128,128]{2,1,0:T(8,128)(2,1)S(1)}, bf16[16,128,128]{2,1,0:T(8,128)(2,1)}, u32[]{:S(2)}, u32[]{:S(2)}) collective-permute-start(bf16[16,128,128]{2,1,0:T(8,128)(2,1)S(1)} %collective-permute-done.rest_3_), channel_id=1, source_target_pairs={{0,8},{8,16},{16,24},{1,9},{9,17},{17,25},{2,10},{10,18},{18,26},{... | collective-permute-start | bytes 1572872 | tf_op jit(solution)/shard_map/ppermute | solution.py:19
  40.9 6.7 %copy-start.6 = (s32[16]{0:T(128)}, s32[16]{0:T(128)S(1)}, u32[]{:S(2)}) copy-start(s32[16]{0:T(128)S(1)} %multiply_add_fusion.place) | copy-start | bytes 196
  41.8 5.8 %copy-start.2 = (bf16[16,128,128]{2,1,0:T(8,128)(2,1)}, bf16[16,128,128]{2,1,0:T(8,128)(2,1)S(1)}, u32[]{:S(2)}) copy-start(bf16[16,128,128]{2,1,0:T(8,128)(2,1)S(1)} %collective-permute-done.2.rest_1_) | copy-start | bytes 1572868
  41.8 5.8 %copy-start.4 = (bf16[16,128,128]{2,1,0:T(8,128)(2,1)}, bf16[16,128,128]{2,1,0:T(8,128)(2,1)S(1)}, u32[]{:S(2)}) copy-start(bf16[16,128,128]{2,1,0:T(8,128)(2,1)S(1)} %collective-permute-done.7.rest_8_) | copy-start | bytes 1572868
  41.8 5.8 %copy-start.5 = (bf16[16,128,128]{2,1,0:T(8,128)(2,1)}, bf16[16,128,128]{2,1,0:T(8,128)(2,1)S(1)}, u32[]{:S(2)}) copy-start(bf16[16,128,128]{2,1,0:T(8,128)(2,1)S(1)} %collective-permute-done.4.rest_2_) | copy-start | bytes 1572868

commit v4 on v3

--- a/solution.py
+++ b/solution.py
@@ -1,5 +1,4 @@
 import functools
-import math
 
 import jax
 import jax.numpy as jnp
@@ -27,8 +26,8 @@
     return (*low, *line, *high)
 
 
-def row_kernel(order, place, count, near, group, a_ref, *rest):
-    pieces, (out_ref, table, sums, sems) = rest[:9], rest[9:]
+def row_kernel(order, place, count, near, group, a_hbm, *rest):
+    pieces, (out_ref, a_ref, table, sums, sems, row_sems) = rest[:9], rest[9:]
     step = pl.program_id(0)
     tiles, rows = a_ref.shape[1], pieces[0].shape[0]
     touched = sums.shape[0]
@@ -41,8 +40,12 @@
         ]
         for copy in copies:
             copy.start()
+        for j in range(rows):
+            pltpu.make_async_copy(a_hbm.at[j], a_ref.at[j], row_sems.at[j]).start()
         for copy in copies:
             copy.wait()
+
+    pltpu.make_async_copy(a_hbm.at[step], a_ref.at[step], row_sems.at[step]).wait()
 
     @pl.when(step < count[0])
     def _():
@@ -50,7 +53,7 @@
         sums[...] = jnp.zeros_like(sums)
         for k in range(tiles):
             product = jnp.dot(
-                a_ref[0, k], table[near[row, k]], preferred_element_type=jnp.float32
+                a_ref[row, k], table[near[row, k]], preferred_element_type=jnp.float32
             )
             sums[group[row, k]] += product
         own = table[4 * rows + row]
@@ -73,19 +76,16 @@
         grid_spec=pltpu.PrefetchScalarGridSpec(
             num_scalar_prefetch=5,
             grid=(steps,),
-            in_specs=[
-                pl.BlockSpec(
-                    (1, tiles, size, size), lambda i, order, *_: (order[i], 0, 0, 0)
-                )
-            ]
-            + [pl.BlockSpec(memory_space=pl.ANY)] * 9,
+            in_specs=[pl.BlockSpec(memory_space=pl.ANY)] * 10,
             out_specs=pl.BlockSpec(
                 (1, touched, size, size), lambda i, order, place, *_: (place[i], 0, 0, 0)
             ),
             scratch_shapes=[
+                pltpu.VMEM(a_local.shape, jnp.bfloat16),
                 pltpu.VMEM((9 * rows, size, size), jnp.bfloat16),
                 pltpu.VMEM((touched, size, size), jnp.float32),
                 pltpu.SemaphoreType.DMA((9,)),
+                pltpu.SemaphoreType.DMA((rows,)),
             ],
         ),
         compiler_params=pltpu.CompilerParams(vmem_limit_bytes=60 << 20),
@@ -95,34 +95,37 @@
     )(order, place, count, near, group, a_local, *pieces)
 
 
-def sum_kernel(segment, valid, recv_ref, out_ref):
+def sum_kernel(segment, valid, recv_hbm, out_ref, recv_ref, sems):
     step = pl.program_id(0)
 
     @pl.when(step == 0)
     def _():
+        for j in range(recv_ref.shape[0]):
+            pltpu.make_async_copy(recv_hbm.at[j], recv_ref.at[j], sems.at[j]).start()
         out_ref[...] = jnp.zeros_like(out_ref)
 
-    batch = recv_ref.shape[0]
-    for j in range(batch):
-        slot = step * batch + j
-
-        @pl.when(valid[slot] > 0)
-        def _():
-            for f in range(recv_ref.shape[1]):
-                out_ref[segment[slot, f]] += recv_ref[j, f].astype(jnp.float32)
+    pltpu.make_async_copy(recv_hbm.at[step], recv_ref.at[step], sems.at[step]).wait()
+
+    @pl.when(valid[step] > 0)
+    def _():
+        for f in range(recv_ref.shape[1]):
+            out_ref[segment[step, f]] += recv_ref[step, f].astype(jnp.float32)
 
 
 def coarse_sums(recv, segment, valid, total):
     slot_total, touched, size, _ = recv.shape
-    batch = math.gcd(slot_total, 4)
     return pl.pallas_call(
         sum_kernel,
         out_shape=jax.ShapeDtypeStruct((total, size, size), jnp.float32),
         grid_spec=pltpu.PrefetchScalarGridSpec(
             num_scalar_prefetch=2,
-            grid=(slot_total // batch,),
-            in_specs=[pl.BlockSpec((batch, touched, size, size), lambda i, *_: (i, 0, 0, 0))],
+            grid=(slot_total,),
+            in_specs=[pl.BlockSpec(memory_space=pl.ANY)],
             out_specs=pl.BlockSpec((total, size, size), lambda i, *_: (0, 0, 0)),
+            scratch_shapes=[
+                pltpu.VMEM(recv.shape, recv.dtype),
+                pltpu.SemaphoreType.DMA((slot_total,)),
+            ],
         ),
         compiler_params=pltpu.CompilerParams(vmem_limit_bytes=60 << 20),
         cost_estimate=pl.CostEstimate(

time: 263 us -> 258 us (0.981)
  Pallas kernels: 212 us -> 208 us
    pallas_call x1, Pallas kernels: 10.3 us -> 7.53 us  [coarse_sums(): pl.pallas_call(sum_kernel, out_shape=jax.ShapeDtypeStruct((total, size, s...]
where the time goes in v4:
time: 258 us
  Pallas kernels  208 us (81%)
  starting transfers between devices  22.4 us (9%)
  waiting for transfers between devices  22 us (9%)
  local copies, waits for them, and re-layouts  3.42 us (1%)
    pallas_call x1, Pallas kernels, swapped(): pl.pallas_call(functools.partial(swap_kernel, count, width), out_shape=(j...  181 us
    ppermute x8, starting transfers between devices, shifted(): return lax.ppermute(block, axis, pairs)  22.4 us
    ppermute x8, waiting for transfers between devices, shifted(): return lax.ppermute(block, axis, pairs)  22 us
    pallas_call x1, Pallas kernels, row_products(): pl.pallas_call(row_kernel, out_shape=jax.ShapeDtypeStruct((slot_total, to...  19.4 us
    pallas_call x1, Pallas kernels, coarse_sums(): pl.pallas_call(sum_kernel, out_shape=jax.ShapeDtypeStruct((total, size, s...  7.53 us
  transfers between devices with their start and end apart: 8, of which 3 were waited for; matrix products, arithmetic and copies ran while one was open for 1% of the time, Pallas kernels for 0%

profile of v4, /device:TPU:9, one launch (start us, length us, event | category | flops | bytes accessed | tf_op | source)
XLA Modules:
  0.0 257.6 jit_solution(15732641676689995687)
XLA Ops:
  0.0 2.6 collective-permute-start.6
  2.6 3.0 %collective-permute-start.3 = (bf16[16,128,128]{2,1,0:T(8,128)(2,1)}, bf16[16,128,128]{2,1,0:T(8,128)(2,1)S(1)}, u32[]{:S(2)}, u32[]{:S(2)}) collective-permute-start(bf16[16,128,128]{2,1,0:T(8,128)(2,1)} %bitcast.26), channel_id=1, source_target_pairs={{1,0},{2,1},{3,2},{4,3},{5,4},{6,5},{7,6},{9,8},{10,9},{11,10},{12... | collective-permute-start | bytes 1572872 | tf_op jit(solution)/shard_map/ppermute | solution.py:18
  5.6 3.3 %collective-permute-start.2 = (bf16[16,128,128]{2,1,0:T(8,128)(2,1)}, bf16[16,128,128]{2,1,0:T(8,128)(2,1)S(1)}, u32[]{:S(2)}, u32[]{:S(2)}) collective-permute-start(bf16[16,128,128]{2,1,0:T(8,128)(2,1)} %bitcast.27), channel_id=1, source_target_pairs={{0,8},{8,16},{16,24},{1,9},{9,17},{17,25},{2,10},{10,18},{18,26},{... | collective-permute-start | bytes 1572872 | tf_op jit(solution)/shard_map/ppermute | solution.py:18
  8.9 2.3 collective-permute-start
  11.2 0.7 fusion.1
  11.9 0.7 bitcast_add_fusion
  12.6 0.2 convert_reduce_fusion
  12.8 16.8 %collective-permute-done.3.rest_5_ = bf16[16,128,128]{2,1,0:T(8,128)(2,1)S(1)} collective-permute-done((bf16[16,128,128]{2,1,0:T(8,128)(2,1)}, bf16[16,128,128]{2,1,0:T(8,128)(2,1)S(1)}, u32[]{:S(2)}, u32[]{:S(2)}) %collective-permute-start.3) | collective-permute-done | bytes 524320 | tf_op jit(solution)/shard_map/ppermute | solution.py:18
  29.6 0.0 copy-start.1
  29.6 2.3 collective-permute-start.7
  31.9 3.4 %collective-permute-start.4 = (bf16[16,128,128]{2,1,0:T(8,128)(2,1)S(1)}, bf16[16,128,128]{2,1,0:T(8,128)(2,1)S(1)}, u32[]{:S(2)}, u32[]{:S(2)}) collective-permute-start(bf16[16,128,128]{2,1,0:T(8,128)(2,1)S(1)} %collective-permute-done.3.rest_5_), channel_id=1, source_target_pairs={{0,8},{8,16},{16,24},{1,9},{9,17},{17,25},{2,10},{10,18},{18,26},{... | collective-permute-start | bytes 1572872 | tf_op jit(solution)/shard_map/ppermute | solution.py:18
  35.3 0.0 collective-permute-done.rest_3_
  35.3 0.0 copy-start.3
  35.3 1.9 collective-permute-start.5
  37.2 0.0 collective-permute-done.6.rest_7_
  37.2 0.0 copy-start
  37.2 3.6 %collective-permute-start.1 = (bf16[16,128,128]{2,1,0:T(8,128)(2,1)S(1)}, bf16[16,128,128]{2,1,0:T(8,128)(2,1)}, u32[]{:S(2)}, u32[]{:S(2)}) collective-permute-start(bf16[16,128,128]{2,1,0:T(8,128)(2,1)S(1)} %collective-permute-done.rest_3_), channel_id=1, source_target_pairs={{0,8},{8,16},{16,24},{1,9},{9,17},{17,25},{2,10},{10,18},{18,26},{... | collective-permute-start | bytes 1572872 | tf_op jit(solution)/shard_map/ppermute | solution.py:18
  40.9 0.0 copy-start.6
  40.9 0.1 iota_compare_fusion
  41.0 0.1 select_reduce_fusion
  41.1 0.1 copy.9
  41.2 0.6 pad.5.meta
  41.8 0.0 collective-permute-done.2.rest_1_
  41.8 0.0 copy-start.2
  41.8 0.0 collective-permute-done.7.rest_8_
  41.8 0.0 copy-start.4
  41.8 0.0 collective-permute-done.4.rest_2_
  41.8 0.0 copy-start.5
  41.8 4.1 %collective-permute-done.5.rest_6_ = bf16[16,128,128]{2,1,0:T(8,128)(2,1)} collective-permute-done((bf16[16,128,128]{2,1,0:T(8,128)(2,1)S(1)}, bf16[16,128,128]{2,1,0:T(8,128)(2,1)}, u32[]{:S(2)}, u32[]{:S(2)}) %collective-permute-start.5) | collective-permute-done | bytes 524320 | tf_op jit(solution)/shard_map/ppermute | solution.py:18
  45.9 1.1 collective-permute-done.1.rest_0_
  47.0 0.6 iota.17.order
  47.6 0.0 copy-done.1
  47.6 0.0 copy-done.3
  47.6 0.0 copy-done
  47.6 0.0 copy-done.6
  47.6 0.0 copy-done.2
  47.6 0.0 copy-done.4
  47.6 0.0 copy-done.5
  47.6 19.4 %shard_map.64.sent = bf16[32,8,128,128]{3,2,1,0:T(8,128)(2,1)} custom-call(s32[16]{0:T(128)} %iota.17.order, s32[16]{0:T(128)} %copy-done.6, s32[1]{0:T(128)} %constant.33.clone.1.count, s32[16,27]{1,0:T(8,128)} %bitcast.33, s32[16,27]{1,0:T(8,128)} %bitcast.34, bf16[16,27,128,128]{3,2,1,0:T(8,128)(2,1)} %bitcast.24, ...), custom_call_target="tpu_custom_call" | custom-call | flops 2348810240 | bytes 18350080 | tf_op jit(solution)/shard_map/pallas_call | solution.py:73
  67.0 180.9 %shard_map.65 = (bf16[32,8,128,128]{3,2,1,0:T(8,128)(2,1)}, s32[8,8,128]{2,1,0:T(8,128)}) custom-call(bf16[32,8,128,128]{3,2,1,0:T(8,128)(2,1)} %shard_map.64.sent, s32[8,8,128]{2,1,0:T(8,128)} %pad.5.meta), custom_call_target="tpu_custom_call" | custom-call | tf_op jit(solution)/shard_map/pallas_call | solution.py:186
  248.0 0.8 slice.9
  248.7 0.7 slice_reduce_fusion.valid
  249.4 0.7 slice.12.segment
  250.1 7.5 %shard_map.66 = f32[108,128,128]{2,1,0:T(8,128)} custom-call(s32[32,8]{1,0:T(8,128)} %slice.12.segment, s32[32]{0:T(128)} %slice_reduce_fusion.valid, bf16[32,8,128,128]{3,2,1,0:T(8,128)(2,1)} %get-tuple-element.8.recv_hbm), custom_call_target="tpu_custom_call" | custom-call | flops 4194304 | bytes 15466496 | tf_op jit(solution)/shard_map/pallas_call | solution.py:117
  (2 shorter events, 0.0 us)
Async XLA Ops:
  0.0 37.2 %collective-permute-start.6 = (bf16[16,128,128]{2,1,0:T(8,128)(2,1)}, bf16[16,128,128]{2,1,0:T(8,128)(2,1)S(1)}, u32[]{:S(2)}, u32[]{:S(2)}) collective-permute-start(bf16[16,128,128]{2,1,0:T(8,128)(2,1)} %bitcast.25), channel_id=1, source_target_pairs={{8,0},{16,8},{24,16},{9,1},{17,9},{25,17},{10,2},{18,10},{26,18},{... | collective-permute-start | bytes 1572872 | tf_op jit(solution)/shard_map/ppermute | solution.py:18
  2.6 27.0 %collective-permute-start.3 = (bf16[16,128,128]{2,1,0:T(8,128)(2,1)}, bf16[16,128,128]{2,1,0:T(8,128)(2,1)S(1)}, u32[]{:S(2)}, u32[]{:S(2)}) collective-permute-start(bf16[16,128,128]{2,1,0:T(8,128)(2,1)} %bitcast.26), channel_id=1, source_target_pairs={{1,0},{2,1},{3,2},{4,3},{5,4},{6,5},{7,6},{9,8},{10,9},{11,10},{12... | collective-permute-start | bytes 1572872 | tf_op jit(solution)/shard_map/ppermute | solution.py:18
  5.6 36.2 %collective-permute-start.2 = (bf16[16,128,128]{2,1,0:T(8,128)(2,1)}, bf16[16,128,128]{2,1,0:T(8,128)(2,1)S(1)}, u32[]{:S(2)}, u32[]{:S(2)}) collective-permute-start(bf16[16,128,128]{2,1,0:T(8,128)(2,1)} %bitcast.27), channel_id=1, source_target_pairs={{0,8},{8,16},{16,24},{1,9},{9,17},{17,25},{2,10},{10,18},{18,26},{... | collective-permute-start | bytes 1572872 | tf_op jit(solution)/shard_map/ppermute | solution.py:18
  8.9 26.3 %collective-permute-start = (bf16[16,128,128]{2,1,0:T(8,128)(2,1)}, bf16[16,128,128]{2,1,0:T(8,128)(2,1)S(1)}, u32[]{:S(2)}, u32[]{:S(2)}) collective-permute-start(bf16[16,128,128]{2,1,0:T(8,128)(2,1)} %bitcast.28), channel_id=1, source_target_pairs={{0,1},{1,2},{2,3},{3,4},{4,5},{5,6},{6,7},{8,9},{9,10},{10,11},{11... | collective-permute-start | bytes 1572872 | tf_op jit(solution)/shard_map/ppermute | solution.py:18
  29.6 18.0 %copy-start.1 = (bf16[16,128,128]{2,1,0:T(8,128)(2,1)}, bf16[16,128,128]{2,1,0:T(8,128)(2,1)S(1)}, u32[]{:S(2)}) copy-start(bf16[16,128,128]{2,1,0:T(8,128)(2,1)S(1)} %collective-permute-done.3.rest_5_) | copy-start | bytes 1572868
  29.6 12.2 %collective-permute-start.7 = (bf16[16,128,128]{2,1,0:T(8,128)(2,1)S(1)}, bf16[16,128,128]{2,1,0:T(8,128)(2,1)S(1)}, u32[]{:S(2)}, u32[]{:S(2)}) collective-permute-start(bf16[16,128,128]{2,1,0:T(8,128)(2,1)S(1)} %collective-permute-done.3.rest_5_), channel_id=1, source_target_pairs={{8,0},{16,8},{24,16},{9,1},{17,9},{25,17},{10,2},{18,10},{26,18},{... | collective-permute-start | bytes 1572872 | tf_op jit(solution)/shard_map/ppermute | solution.py:18
  31.9 9.9 %collective-permute-start.4 = (bf16[16,128,128]{2,1,0:T(8,128)(2,1)S(1)}, bf16[16,128,128]{2,1,0:T(8,128)(2,1)S(1)}, u32[]{:S(2)}, u32[]{:S(2)}) collective-permute-start(bf16[16,128,128]{2,1,0:T(8,128)(2,1)S(1)} %collective-permute-done.3.rest_5_), channel_id=1, source_target_pairs={{0,8},{8,16},{16,24},{1,9},{9,17},{17,25},{2,10},{10,18},{18,26},{... | collective-permute-start | bytes 1572872 | tf_op jit(solution)/shard_map/ppermute | solution.py:18
  35.3 12.3 %copy-start.3 = (bf16[16,128,128]{2,1,0:T(8,128)(2,1)}, bf16[16,128,128]{2,1,0:T(8,128)(2,1)S(1)}, u32[]{:S(2)}) copy-start(bf16[16,128,128]{2,1,0:T(8,128)(2,1)S(1)} %collective-permute-done.rest_3_) | copy-start | bytes 1572868
  35.3 10.6 %collective-permute-start.5 = (bf16[16,128,128]{2,1,0:T(8,128)(2,1)S(1)}, bf16[16,128,128]{2,1,0:T(8,128)(2,1)}, u32[]{:S(2)}, u32[]{:S(2)}) collective-permute-start(bf16[16,128,128]{2,1,0:T(8,128)(2,1)S(1)} %collective-permute-done.rest_3_), channel_id=1, source_target_pairs={{8,0},{16,8},{24,16},{9,1},{17,9},{25,17},{10,2},{18,10},{26,18},{... | collective-permute-start | bytes 1572872 | tf_op jit(solution)/shard_map/ppermute | solution.py:18
  37.2 10.3 %copy-start = (bf16[16,128,128]{2,1,0:T(8,128)(2,1)}, bf16[16,128,128]{2,1,0:T(8,128)(2,1)S(1)}, u32[]{:S(2)}) copy-start(bf16[16,128,128]{2,1,0:T(8,128)(2,1)S(1)} %collective-permute-done.6.rest_7_) | copy-start | bytes 1572868
  37.2 9.8 %collective-permute-start.1 = (bf16[16,128,128]{2,1,0:T(8,128)(2,1)S(1)}, bf16[16,128,128]{2,1,0:T(8,128)(2,1)}, u32[]{:S(2)}, u32[]{:S(2)}) collective-permute-start(bf16[16,128,128]{2,1,0:T(8,128)(2,1)S(1)} %collective-permute-done.rest_3_), channel_id=1, source_target_pairs={{0,8},{8,16},{16,24},{1,9},{9,17},{17,25},{2,10},{10,18},{18,26},{... | collective-permute-start | bytes 1572872 | tf_op jit(solution)/shard_map/ppermute | solution.py:18
  40.9 6.7 %copy-start.6 = (s32[16]{0:T(128)}, s32[16]{0:T(128)S(1)}, u32[]{:S(2)}) copy-start(s32[16]{0:T(128)S(1)} %multiply_add_fusion.place) | copy-start | bytes 196
  41.8 5.8 %copy-start.2 = (bf16[16,128,128]{2,1,0:T(8,128)(2,1)}, bf16[16,128,128]{2,1,0:T(8,128)(2,1)S(1)}, u32[]{:S(2)}) copy-start(bf16[16,128,128]{2,1,0:T(8,128)(2,1)S(1)} %collective-permute-done.2.rest_1_) | copy-start | bytes 1572868
  41.8 5.8 %copy-start.4 = (bf16[16,128,128]{2,1,0:T(8,128)(2,1)}, bf16[16,128,128]{2,1,0:T(8,128)(2,1)S(1)}, u32[]{:S(2)}) copy-start(bf16[16,128,128]{2,1,0:T(8,128)(2,1)S(1)} %collective-permute-done.7.rest_8_) | copy-start | bytes 1572868
  41.8 5.8 %copy-start.5 = (bf16[16,128,128]{2,1,0:T(8,128)(2,1)}, bf16[16,128,128]{2,1,0:T(8,128)(2,1)S(1)}, u32[]{:S(2)}) copy-start(bf16[16,128,128]{2,1,0:T(8,128)(2,1)S(1)} %collective-permute-done.4.rest_2_) | copy-start | bytes 1572868
